TPU v7x, 32 devices: a whole 2x2x4 slice. The times are simulated.
32 devices in a mesh: runs: 2 (over x), sec: 16 (over z, y, core).
Axes of the slice: x: 2, y: 2, z: 4, core: 2. Of those that a mesh axis runs over, the one named last changes fastest.
Arguments:
- edge_rows: bfloat16 [4096, 1024], P(('runs', 'sec')), parts along dimension 0, may hold values from -46 to 46
- corner: bfloat16 [32768, 1024], P(('runs', 'sec')), parts along dimension 0, may hold values from -1 to 2.2
- joining: int32 [32, 16], P('runs'), parts along dimension 0, may hold values from 0 to 15, as said below
- charge_left: int32 [4096], P(('runs', 'sec')), parts along dimension 0, may hold values from 0 to 15
- charge_right: int32 [4096], P(('runs', 'sec')), parts along dimension 0, may hold values from 0 to 15
Outputs:
- isometry: float32 [4096, 1024], P(('runs', 'sec')), parts along dimension 0
There are 2 independent parts, one for each index of `runs`. A program takes and returns all parts, laid end to end along the dimension named above; each array names one. Nothing has to cross between parts.
Inputs may be any that keep to these rules, and one draw needn't show every extreme that they name: joining[charge_left[e], charge_right[e]] names the block that row e needs; each row of joining names every block once; among the 128 rows of one device at most 16 need the same block, and one block, drawn per copy, receives exactly 16 rows from every device.
All inputs are finite; a program needn't handle non-finite values.
Results may differ from a plain program's by a relative error of at most 0.0003.
Values may be sent and summed in bfloat16 or wider, within the bound.
A program may use at most 128 MiB of HBM per device.

v0:
```python
import math

import jax
import jax.numpy as jnp
from jax import lax
from jax.sharding import PartitionSpec as P


def gram_of(images):
    return lax.dot_general(
        images, images, (((0,), (0,)), ((), ())), precision=lax.Precision.HIGHEST
    )


def reduce_gram(partial_gram):
    return lax.psum(partial_gram, "sec")


def solve_rows(gram_total, images, factor):
    lower = jnp.linalg.cholesky(gram_total)
    solved = lax.linalg.triangular_solve(
        lower, images, left_side=False, lower=True, transpose_a=True
    )
    return solved * factor


def per_device(edge_rows, corner, joining, charge_left, charge_right):
    row_count, feature_len = edge_rows.shape
    owners = lax.axis_size("sec")
    capacity = 2 * row_count // owners
    factor = math.sqrt(row_count * owners)
    target = joining[charge_left, charge_right]
    labels = jnp.arange(owners, dtype=jnp.int32)
    onehot = (target[:, None] == labels[None, :]).astype(jnp.int32)
    before = jnp.cumsum(onehot, axis=0) - onehot
    order_in = jnp.sum(before * onehot, axis=1)
    slot_index = target * capacity + order_in
    packed = (
        jnp.zeros((owners * capacity, feature_len), edge_rows.dtype).at[slot_index].set(edge_rows)
    )
    arrived = lax.all_to_all(
        packed.reshape(owners, capacity, feature_len),
        "sec",
        split_axis=0,
        concat_axis=0,
        tiled=True,
    )
    product = jnp.dot(
        arrived.reshape(owners * capacity, feature_len), corner, preferred_element_type=jnp.float32
    )
    returned = lax.all_to_all(
        product.reshape(owners, capacity, feature_len),
        "sec",
        split_axis=0,
        concat_axis=0,
        tiled=True,
    )
    home_rows = returned.reshape(owners * capacity, feature_len)[slot_index]
    gram_total = reduce_gram(gram_of(home_rows))
    result = solve_rows(gram_total, home_rows, factor)
    return result


def solution(mesh):
    placed = (
        P(("runs", "sec"), None),
        P(("runs", "sec"), None),
        P("runs", None),
        P(("runs", "sec")),
        P(("runs", "sec")),
    )
    return jax.shard_map(
        per_device, mesh=mesh, in_specs=placed, out_specs=P(("runs", "sec"), None), check_vma=False
    )
```

profile of v0, /device:TPU:0, one launch (start us, length us, event | category | flops | bytes accessed | tf_op | source)
XLA Modules:
  0.0 532.5 jit_solution(10985662273501543571)
XLA Ops:
  7.4 1.8 gather_fusion
  9.6 1.7 scatter_custom_fusion
  11.4 21.7 %all_to_all.10 = bf16[16,16,1024]{2,1,0:T(8,128)(2,1)S(1)} all-to-all(bf16[16,16,1024]{2,1,0:T(8,128)(2,1)S(1)} %bitcast.114), channel_id=1, replica_groups=mesh['runs'=2,'sec'=16] {'sec'}, dimensions={0} | all-to-all | bytes 1048576 | tf_op jit(solution)/shard_map/all_to_all | solution.py:41
  33.0 1.7 fusion.1
  34.7 4.1 all-to-all-start.1
  38.9 22.9 %all-to-all-done.1 = f32[16,16,1024]{2,1,0:T(8,128)S(1)} async-done(((f32[16,16,1024]{2,1,0:T(8,128)}), f32[16,16,1024]{2,1,0:T(8,128)S(1)}, u32[]{:S(2)}, u32[]{:S(2)}) %all-to-all-start.1) | async-done | bytes 1048608 | tf_op jit(solution)/shard_map/all_to_all | solution.py:51
  63.3 6.6 %fusion.73 = f32[1024,1024]{0,1:T(8,128)} fusion(f32[128,1024]{1,0:T(8,128)} %gather_fusion.1), kind=kOutput, calls=%fused_computation.176 | convolution fusion | flops 1610612736 | bytes 4718592 | tf_op jit(solution)/shard_map/dot_general | solution.py:10
  70.0 113.8 %all-reduce.3.cloned.1.call-done = f32[1024,1024]{0,1:T(8,128)} async-done(((f32[1024,1024]{0,1:T(8,128)}), f32[1024,1024]{0,1:T(8,128)}) %all-reduce.3.cloned.1.call-update) | async-done | bytes 4194320 | tf_op jit(solution)/shard_map/psum | solution.py:16
  183.8 5.8 %copy.10 = f32[1024,1024]{1,0:T(8,128)} copy(f32[1024,1024]{0,1:T(8,128)} %all-reduce.3.cloned.1.call-done) | data formatting | bytes 8388608 | tf_op jit(solution)/shard_map/psum | solution.py:16
  189.6 4.4 fusion
  194.1 1.9 copy-done.1
  196.0 11.7 %cholesky.223 = f32[128,128]{1,0:T(8,128)S(1)} custom-call(f32[128,128]{1,0:T(8,128)S(1)} %cholesky.580), custom_call_target="Cholesky" | custom-call | tf_op jit(solution)/shard_map/jit(cholesky)/cholesky | solution.py:20
  207.8 9.8 %custom-call.62 = f32[1,128,128]{1,2,0:T(8,128)S(1)} custom-call(f32[1,128,128]{2,1,0:T(8,128)S(1)} %get-tuple-element.69), custom_call_target="InvertDiagBlocksLowerTriangular" | custom-call | tf_op jit(solution)/shard_map/jit(cholesky)/cholesky | solution.py:20
  217.6 2.5 cholesky.255
  220.1 2.4 constant_dynamic-update-slice_fusion.31
  224.0 11.9 %cholesky.244 = f32[128,128]{1,0:T(8,128)S(1)} custom-call(f32[128,128]{1,0:T(8,128)S(1)} %cholesky.584), custom_call_target="Cholesky" | custom-call | tf_op jit(solution)/shard_map/jit(cholesky)/cholesky | solution.py:20
  236.5 9.8 %custom-call.63 = f32[1,128,128]{1,2,0:T(8,128)S(1)} custom-call(f32[1,128,128]{2,1,0:T(8,128)S(1)} %get-tuple-element.66), custom_call_target="InvertDiagBlocksLowerTriangular" | custom-call | tf_op jit(solution)/shard_map/jit(cholesky)/cholesky | solution.py:20
  247.6 2.1 convolution_subtract_fusion.1
  249.7 11.7 %cholesky.468 = f32[128,128]{1,0:T(8,128)S(1)} custom-call(f32[128,128]{1,0:T(8,128)S(1)} %cholesky.589), custom_call_target="Cholesky" | custom-call | tf_op jit(solution)/shard_map/jit(cholesky)/cholesky | solution.py:20
  262.7 9.8 %custom-call.64 = f32[1,128,128]{1,2,0:T(8,128)S(1)} custom-call(f32[1,128,128]{2,1,0:T(8,128)S(1)} %get-tuple-element.63), custom_call_target="InvertDiagBlocksLowerTriangular" | custom-call | tf_op jit(solution)/shard_map/jit(cholesky)/cholesky | solution.py:20
  273.7 2.3 convolution_subtract_fusion.2
  276.1 11.9 %cholesky.487 = f32[128,128]{1,0:T(8,128)S(1)} custom-call(f32[128,128]{1,0:T(8,128)S(1)} %cholesky.594), custom_call_target="Cholesky" | custom-call | tf_op jit(solution)/shard_map/jit(cholesky)/cholesky | solution.py:20
  289.2 9.8 %custom-call.65 = f32[1,128,128]{1,2,0:T(8,128)S(1)} custom-call(f32[1,128,128]{2,1,0:T(8,128)S(1)} %get-tuple-element.60), custom_call_target="InvertDiagBlocksLowerTriangular" | custom-call | tf_op jit(solution)/shard_map/jit(cholesky)/cholesky | solution.py:20
  300.2 2.3 convolution_subtract_fusion.3
  302.5 11.7 %cholesky.506 = f32[128,128]{1,0:T(8,128)S(1)} custom-call(f32[128,128]{1,0:T(8,128)S(1)} %cholesky.599), custom_call_target="Cholesky" | custom-call | tf_op jit(solution)/shard_map/jit(cholesky)/cholesky | solution.py:20
  315.5 10.2 %custom-call.66 = f32[1,128,128]{1,2,0:T(8,128)S(1)} custom-call(f32[1,128,128]{2,1,0:T(8,128)S(1)} %get-tuple-element.57), custom_call_target="InvertDiagBlocksLowerTriangular" | custom-call | tf_op jit(solution)/shard_map/jit(cholesky)/cholesky | solution.py:20
  326.7 2.3 convolution_subtract_fusion.4
  329.0 11.7 %cholesky.526 = f32[128,128]{1,0:T(8,128)S(1)} custom-call(f32[128,128]{1,0:T(8,128)S(1)} %cholesky.604), custom_call_target="Cholesky" | custom-call | tf_op jit(solution)/shard_map/jit(cholesky)/cholesky | solution.py:20
  342.0 9.8 %custom-call.67 = f32[1,128,128]{1,2,0:T(8,128)S(1)} custom-call(f32[1,128,128]{2,1,0:T(8,128)S(1)} %get-tuple-element.54), custom_call_target="InvertDiagBlocksLowerTriangular" | custom-call | tf_op jit(solution)/shard_map/jit(cholesky)/cholesky | solution.py:20
  352.8 2.0 convolution_subtract_fusion.5
  354.8 11.9 %cholesky.546 = f32[128,128]{1,0:T(8,128)S(1)} custom-call(f32[128,128]{1,0:T(8,128)S(1)} %cholesky.609), custom_call_target="Cholesky" | custom-call | tf_op jit(solution)/shard_map/jit(cholesky)/cholesky | solution.py:20
  367.9 9.8 %custom-call.68 = f32[1,128,128]{1,2,0:T(8,128)S(1)} custom-call(f32[1,128,128]{2,1,0:T(8,128)S(1)} %get-tuple-element.51), custom_call_target="InvertDiagBlocksLowerTriangular" | custom-call | tf_op jit(solution)/shard_map/jit(cholesky)/cholesky | solution.py:20
  378.6 1.8 convolution_subtract_fusion.11
  380.4 11.7 %cholesky.564 = f32[128,128]{1,0:T(8,128)S(1)} custom-call(f32[128,128]{1,0:T(8,128)S(1)} %convolution_subtract_fusion.11), custom_call_target="Cholesky" | custom-call | tf_op jit(solution)/shard_map/jit(cholesky)/cholesky | solution.py:20
  399.0 4.8 select_select_fusion
  403.9 27.6 %while.1 = (s32[]{:T(128)}, f32[1024,1024]{1,0:T(8,128)}, s32[8,2]{0,1:T(2,128)S(1)}, f32[8,128,128]{2,1,0:T(8,128)}, s32[]{:T(128)}) while((s32[]{:T(128)}, f32[1024,1024]{1,0:T(8,128)}, s32[8,2]{0,1:T(2,128)S(1)}, f32[8,128,128]{2,1,0:T(8,128)}, s32[]{:T(128)}) %tuple.57), condition=%wide.while_cond, body=%wide.while_body.sunk | while | flops 2 | bytes 132705 | solution.py:21
  404.5 2.9 bitcast_dynamic-update-slice_fusion.2
  408.0 2.8 bitcast_dynamic-update-slice_fusion.2
  411.4 2.8 bitcast_dynamic-update-slice_fusion.2
  414.9 2.8 bitcast_dynamic-update-slice_fusion.2
  418.4 2.8 bitcast_dynamic-update-slice_fusion.2
  421.8 2.8 bitcast_dynamic-update-slice_fusion.2
  425.3 2.8 bitcast_dynamic-update-slice_fusion.2
  428.7 2.8 bitcast_dynamic-update-slice_fusion.2
  431.5 79.6 %custom-call.69 = f32[8,128,128]{1,2,0:T(8,128)S(1)} custom-call(f32[8,128,128]{2,1,0:T(8,128)} %get-tuple-element.12), custom_call_target="InvertDiagBlocksLowerTriangular" | custom-call | tf_op jit(solution)/shard_map/triangular_solve | solution.py:21
  518.0 1.7 convolution_subtract_fusion.8
  520.0 1.8 convolution_subtract_fusion.7
  522.1 1.9 convolution_subtract_fusion.6
  (76 shorter events, 33.7 us)
Async XLA Ops:
  6.5 26.5 %copy-start = (bf16[1024,1024]{1,0:T(8,128)(2,1)S(1)}, bf16[1024,1024]{1,0:T(8,128)(2,1)}, u32[]{:S(2)}) copy-start(bf16[1024,1024]{1,0:T(8,128)(2,1)} %param.6) | copy-start | bytes 6291460
  34.7 27.0 %all-to-all-start.1 = ((f32[16,16,1024]{2,1,0:T(8,128)}), f32[16,16,1024]{2,1,0:T(8,128)S(1)}, u32[]{:S(2)}, u32[]{:S(2)}) async-start(f32[16,16,1024]{2,1,0:T(8,128)} %fusion.1), calls=%async_computation.1 | async-start | bytes 2097152 | tf_op jit(solution)/shard_map/all_to_all | solution.py:51
  38.8 145.0 %all-reduce.3.cloned.1.call-start = ((), (), s32[]{:S(2)}) async-start(), calls=%async_computation.2 | async-start | bytes 8388608 | tf_op jit(solution)/shard_map/psum | solution.py:16
  194.1 1.9 copy-start.1
  399.0 112.1 %copy-start.2 = (f32[128,1024]{1,0:T(8,128)S(1)}, f32[128,1024]{1,0:T(8,128)}, u32[]{:S(2)}) copy-start(f32[128,1024]{1,0:T(8,128)} %gather_fusion.1) | copy-start | bytes 1572868
Sparse Core Ops, SparseCore 0:
  70.1 113.6 all-reduce.2
where the time goes:
time: 539 us; the launch traced here: 533 us
  other arithmetic  263 us (49%)
  waiting for transfers between devices  137 us (25%)
  matrix products  44.5 us (8%)
  local copies, waits for them, and re-layouts  44.1 us (8%)
  blocking collectives  21.7 us (4%)
  between operations  18.9 us (4%)
    another operation x30, other arithmetic, solve_rows(): lower = jnp.linalg.cholesky(gram_total)  172 us
    psum x1, waiting for transfers between devices, reduce_gram(): return lax.psum(partial_gram, 'sec')  114 us
    another operation x3, other arithmetic, solve_rows(): lax.linalg.triangular_solve(lower, images, left_side=False, lower=True, t...  84.5 us
    another operation x24, local copies, waits for them, and re-layouts  27.6 us
    another operation x14, matrix products, solve_rows(): lower = jnp.linalg.cholesky(gram_total)  23.1 us
    all_to_all x1, waiting for transfers between devices, per_device(): lax.all_to_all(product.reshape(owners, capacity, feature_len), 'sec', spl...  22.9 us
    all_to_all x1, blocking collectives, per_device(): lax.all_to_all(packed.reshape(owners, capacity, feature_len), 'sec', spli...  21.7 us
    another operation x15, matrix products, solve_rows(): lax.linalg.triangular_solve(lower, images, left_side=False, lower=True, t...  13.1 us
  transfers between devices with their start and end apart: 2, of which 2 were waited for; matrix products, arithmetic and copies ran while one was open for 0% of the time, Pallas kernels for 0%

commit v1 on v0

--- a/solution.py
+++ b/solution.py
@@ -3,25 +3,151 @@
 import jax
 import jax.numpy as jnp
 from jax import lax
+from jax.experimental import pallas as pl
+from jax.experimental.pallas import tpu as pltpu
 from jax.sharding import PartitionSpec as P
 
-
-def gram_of(images):
-    return lax.dot_general(
-        images, images, (((0,), (0,)), ((), ())), precision=lax.Precision.HIGHEST
-    )
+B = 128
+S = 8
+F32 = jnp.float32
+BF16 = jnp.bfloat16
 
 
-def reduce_gram(partial_gram):
-    return lax.psum(partial_gram, "sec")
+def split2(x):
+    hi = x.astype(BF16)
+    lo = (x - hi.astype(F32)).astype(BF16)
+    return hi, lo
 
 
-def solve_rows(gram_total, images, factor):
-    lower = jnp.linalg.cholesky(gram_total)
-    solved = lax.linalg.triangular_solve(
-        lower, images, left_side=False, lower=True, transpose_a=True
-    )
-    return solved * factor
+def starts(nb):
+    offs, at = [], 0
+    for j in range(nb):
+        offs.append(at)
+        at += (nb - j) * B
+    return offs, at
+
+
+def dot(a, b, dims):
+    return lax.dot_general(a, b, (dims, ((), ())), preferred_element_type=F32)
+
+
+def product_kernel(nb, rows_ref, corner_ref, image_ref, gram_ref):
+    image = dot(rows_ref[...], corner_ref[...], ((1,), (0,)))
+    image_ref[...] = image
+    hi, lo = split2(image)
+    left = jnp.concatenate([hi, hi, lo], axis=0).T
+    right = jnp.concatenate([hi, lo, hi], axis=0)
+    offs, _ = starts(nb)
+    for j in range(nb):
+        gram_ref[pl.ds(offs[j], (nb - j) * B), :] = dot(
+            left[j * B :, :], right[:, j * B : (j + 1) * B], ((1,), (0,))
+        )
+
+
+def factor_block(t_ref):
+    row8 = lax.broadcasted_iota(jnp.int32, (S, B), 0)
+    lane = lax.broadcasted_iota(jnp.int32, (S, B), 1)
+    rowb = lax.broadcasted_iota(jnp.int32, (B, 2 * B), 0)
+
+    def step(i, carry):
+        at = pl.multiple_of(i * S, S)
+        v0 = t_ref[pl.ds(at, S), :B]
+        v1 = t_ref[pl.ds(at, S), B:]
+        turned = pltpu.roll(v0, lax.rem(B - at, B), 1)
+        cols = [jnp.broadcast_to(turned[:, m : m + 1], (S, B)) for m in range(S)]
+        scale = jnp.zeros((S, B), F32)
+        for j in range(S):
+            pivot = cols[j][j : j + 1, :]
+            f = jnp.where(row8 > j, cols[j] * (1.0 / pivot), 0.0)
+            scale = jnp.where(row8 == j, lax.rsqrt(pivot), scale)
+            for m in range(j + 1, S):
+                cols[m] = cols[m] - f * cols[m][j : j + 1, :]
+            v0 = v0 - f * v0[j : j + 1, :]
+            v1 = v1 - f * v1[j : j + 1, :]
+        v0 = v0 * scale
+        v1 = v1 * scale
+        u = jnp.where(lane >= at + S, v0, 0.0)
+        uh = u.astype(BF16).astype(F32)
+        um = (u - uh).astype(BF16).astype(F32)
+        ul = u - uh - um
+        v = jnp.concatenate([v0, v1], axis=1)
+        vh = v.astype(BF16).astype(F32)
+        vm = (v - vh).astype(BF16).astype(F32)
+        vl = v - vh - vm
+        lhs = jnp.concatenate([uh, uh, um, um, uh, ul], axis=0).astype(BF16)
+        rhs = jnp.concatenate([vh, vm, vh, vm, vl, vh], axis=0).astype(BF16)
+        change = dot(lhs, rhs, ((0,), (0,)))
+        t_ref[...] = t_ref[...] - change
+        t_ref[pl.ds(at, S), B:] = v1
+        return carry
+
+    lax.fori_loop(0, B // S, step, 0)
+
+
+def solve_kernel(nb, factor, gram_ref, home_ref, out_ref, a_ref, t_ref):
+    offs, total = starts(nb)
+    rows = home_ref.shape[0]
+    a_ref[...] = gram_ref[...]
+    out_ref[...] = home_ref[...]
+    eye = (
+        lax.broadcasted_iota(jnp.int32, (B, B), 0) == lax.broadcasted_iota(jnp.int32, (B, B), 1)
+    ).astype(F32)
+    for k in range(nb):
+        t_ref[:, :B] = a_ref[pl.ds(offs[k], B), :]
+        t_ref[:, B:] = eye
+        factor_block(t_ref)
+        ih, il = split2(t_ref[:, B:])
+        inv = jnp.concatenate([ih, il, ih], axis=1)
+        below = (nb - k - 1) * B
+        x = out_ref[:, k * B : (k + 1) * B]
+        if below:
+            x = jnp.concatenate([a_ref[pl.ds(offs[k] + B, below), :], x], axis=0)
+        xh, xl = split2(x)
+        panel = dot(jnp.concatenate([xh, xh, xl], axis=1), inv, ((1,), (1,)))
+        out_ref[:, k * B : (k + 1) * B] = panel[below:, :] * factor
+        if below:
+            ph, plo = split2(panel)
+            left = jnp.concatenate([ph, ph, plo], axis=1)
+            right = jnp.concatenate([ph, plo, ph], axis=1)
+            for j in range(k + 1, nb):
+                at = (j - k - 1) * B
+                change = dot(left[at:, :], right[at : at + B, :], ((1,), (1,)))
+                size = (nb - j) * B
+                a_ref[pl.ds(offs[j], size), :] = a_ref[pl.ds(offs[j], size), :] - change[:size, :]
+                out_ref[:, j * B : (j + 1) * B] = (
+                    out_ref[:, j * B : (j + 1) * B] - change[size:, :]
+                )
+
+
+def products(rows, corner):
+    nb = corner.shape[1] // B
+    _, total = starts(nb)
+    vmem = pl.BlockSpec(memory_space=pltpu.VMEM)
+    return pl.pallas_call(
+        lambda *refs: product_kernel(nb, *refs),
+        out_shape=(
+            jax.ShapeDtypeStruct((rows.shape[0], corner.shape[1]), F32),
+            jax.ShapeDtypeStruct((total, B), F32),
+        ),
+        in_specs=[vmem, vmem],
+        out_specs=(vmem, vmem),
+        compiler_params=pltpu.CompilerParams(vmem_limit_bytes=48 << 20),
+        name="products",
+    )(rows, corner)
+
+
+def solve_rows(gram, home, factor):
+    nb = home.shape[1] // B
+    vmem = pl.BlockSpec(memory_space=pltpu.VMEM)
+    return pl.pallas_call(
+        lambda *refs: solve_kernel(nb, factor, *refs),
+        out_shape=jax.ShapeDtypeStruct(home.shape, F32),
+        in_specs=[vmem, vmem],
+        out_specs=vmem,
+        scratch_shapes=[pltpu.VMEM(gram.shape, F32), pltpu.VMEM((B, 2 * B), F32)],
+        compiler_params=pltpu.CompilerParams(vmem_limit_bytes=48 << 20),
+        name="solve_rows",
+    )(gram, home)
 
 
 def per_device(edge_rows, corner, joining, charge_left, charge_right):
@@ -45,9 +171,8 @@
         concat_axis=0,
         tiled=True,
     )
-    product = jnp.dot(
-        arrived.reshape(owners * capacity, feature_len), corner, preferred_element_type=jnp.float32
-    )
+    product, gram_part = products(arrived.reshape(owners * capacity, feature_len), corner)
+    gram = lax.psum(gram_part, "sec")
     returned = lax.all_to_all(
         product.reshape(owners, capacity, feature_len),
         "sec",
@@ -56,9 +181,7 @@
         tiled=True,
     )
     home_rows = returned.reshape(owners * capacity, feature_len)[slot_index]
-    gram_total = reduce_gram(gram_of(home_rows))
-    result = solve_rows(gram_total, home_rows, factor)
-    return result
+    return solve_rows(gram, home_rows, factor)
 
 
 def solution(mesh):

time: 539 us -> 227 us (0.42); the launches traced: 533 us -> 227 us
  other arithmetic: 263 us -> 1.27 us
  Pallas kernels: 0 us -> 68.1 us
  matrix products: 44.5 us -> 0 us
  local copies, waits for them, and re-layouts: 44.1 us -> 5.47 us
  waiting for transfers between devices: 137 us -> 113 us
  between operations: 18.9 us -> 13.5 us
    another operation x33 -> x0, other arithmetic: 257 us -> none  [the longest x30 172 us: solve_rows(): lower = jnp.linalg.cholesky(gram_total)]
    pallas_call x0 -> x2, Pallas kernels: none -> 68.1 us  [the longest x1 64.1 us: solve_rows(): pl.pallas_call(lambda *refs: solve_kernel(nb, factor, *refs), out_shape=j...]
    another operation x29 -> x0, matrix products: 36.2 us -> none  [the longest x14 23.1 us: solve_rows(): lower = jnp.linalg.cholesky(gram_total)]
    another operation x33 -> x0, local copies, waits for them, and re-layouts: 30.2 us -> none
    psum x1, waiting for transfers between devices: 114 us -> 84.3 us  [per_device(): gram = lax.psum(gram_part, 'sec')]
    dot_general x2 -> x0, matrix products: 8.34 us -> none  [the longest x1 6.64 us: gram_of(): lax.dot_general(images, images, (((0,), (0,)), ((), ())), precision=lax.P...]
    psum x1 -> x0, local copies, waits for them, and re-layouts: 5.84 us -> none  [reduce_gram(): return lax.psum(partial_gram, 'sec')]
where the time goes in v1:
time: 227 us
  waiting for transfers between devices  113 us (50%)
  Pallas kernels  68.1 us (30%)
  blocking collectives  21.7 us (10%)
  between operations  13.5 us (6%)
  local copies, waits for them, and re-layouts  5.47 us (2%)
  starting transfers between devices  4.13 us (2%)
    psum x1, waiting for transfers between devices, per_device(): gram = lax.psum(gram_part, 'sec')  84.3 us
    pallas_call x1, Pallas kernels, solve_rows(): pl.pallas_call(lambda *refs: solve_kernel(nb, factor, *refs), out_shape=j...  64.1 us
    all_to_all x1, waiting for transfers between devices, per_device(): lax.all_to_all(product.reshape(owners, capacity, feature_len), 'sec', spl...  27.6 us
    all_to_all x1, blocking collectives, per_device(): lax.all_to_all(packed.reshape(owners, capacity, feature_len), 'sec', spli...  21.7 us
  transfers between devices with their start and end apart: 2, of which 2 were waited for; matrix products, arithmetic and copies ran while one was open for 0% of the time, Pallas kernels for 0%

profile of v1, /device:TPU:0, one launch (start us, length us, event | category | flops | bytes accessed | tf_op | source)
XLA Modules:
  0.0 226.7 jit_solution(16274221298434196114)
XLA Ops:
  6.5 0.0 copy-start
  6.5 0.0 copy-start.2
  6.5 0.8 fusion.5
  7.4 0.0 copy-done
  7.4 1.3 gather_fusion
  8.6 0.1 fusion.2
  8.7 0.2 reduce_window_sum.11
  8.9 0.2 select_reduce_fusion
  9.1 1.7 scatter_custom_fusion
  10.8 21.7 %all_to_all.10 = bf16[16,16,1024]{2,1,0:T(8,128)(2,1)S(1)} all-to-all(bf16[16,16,1024]{2,1,0:T(8,128)(2,1)S(1)} %bitcast.10), channel_id=1, replica_groups=mesh['runs'=2,'sec'=16] {'sec'}, dimensions={0} | all-to-all | bytes 1048576 | tf_op jit(solution)/shard_map/all_to_all | solution.py:167
  32.5 0.0 copy-done.2
  32.5 4.0 %products.1 = (f32[256,1024]{1,0:T(8,128)}, f32[4608,128]{1,0:T(8,128)}) custom-call(bf16[256,1024]{1,0:T(8,128)(2,1)S(1)} %bitcast.8, bf16[1024,1024]{1,0:T(8,128)(2,1)S(1)} %copy-done.2), custom_call_target="tpu_custom_call" | custom-call | tf_op jit(solution)/shard_map/products/pallas_call | solution.py:126
  36.5 4.1 %all-to-all-start.1 = ((f32[16,16,1024]{2,1,0:T(8,128)}), f32[16,16,1024]{2,1,0:T(8,128)S(1)}, u32[]{:S(2)}, u32[]{:S(2)}) async-start(f32[16,16,1024]{2,1,0:T(8,128)} %bitcast.4), calls=%async_computation.1 | async-start | bytes 2097152 | tf_op jit(solution)/shard_map/all_to_all | solution.py:176
  40.6 0.0 all-reduce.2.cloned.1.call-start
  40.7 0.7 all-reduce.2.cloned.1.call-update
  41.4 27.6 %all-to-all-done.1 = f32[16,16,1024]{2,1,0:T(8,128)S(1)} async-done(((f32[16,16,1024]{2,1,0:T(8,128)}), f32[16,16,1024]{2,1,0:T(8,128)S(1)}, u32[]{:S(2)}, u32[]{:S(2)}) %all-to-all-start.1) | async-done | bytes 1048608 | tf_op jit(solution)/shard_map/all_to_all | solution.py:176
  69.0 0.8 gather_fusion.1
  69.8 84.3 %all-reduce.2.cloned.1.call-done.refs_0_ = f32[4608,128]{1,0:T(8,128)} async-done(((f32[4608,128]{1,0:T(8,128)}), f32[4608,128]{1,0:T(8,128)}) %all-reduce.2.cloned.1.call-update) | async-done | bytes 2359312 | tf_op jit(solution)/shard_map/psum | solution.py:175
  154.1 0.0 copy-start.1
  154.1 1.7 copy-done.1
  155.7 64.1 %solve_rows.1 = f32[128,1024]{1,0:T(8,128)} custom-call(f32[4608,128]{1,0:T(8,128)S(1)} %copy-done.1, f32[128,1024]{1,0:T(8,128)S(1)} %gather_fusion.1), custom_call_target="tpu_custom_call" | custom-call | tf_op jit(solution)/shard_map/solve_rows/pallas_call | solution.py:142
  (2 shorter events, 0.0 us)
Async XLA Ops:
  6.5 0.8 copy-start
  6.5 26.0 %copy-start.2 = (bf16[1024,1024]{1,0:T(8,128)(2,1)S(1)}, bf16[1024,1024]{1,0:T(8,128)(2,1)}, u32[]{:S(2)}) copy-start(bf16[1024,1024]{1,0:T(8,128)(2,1)} %refs_1_.1) | copy-start | bytes 6291460
  36.5 32.5 %all-to-all-start.1 = ((f32[16,16,1024]{2,1,0:T(8,128)}), f32[16,16,1024]{2,1,0:T(8,128)S(1)}, u32[]{:S(2)}, u32[]{:S(2)}) async-start(f32[16,16,1024]{2,1,0:T(8,128)} %bitcast.4), calls=%async_computation.1 | async-start | bytes 2097152 | tf_op jit(solution)/shard_map/all_to_all | solution.py:176
  40.6 113.4 %all-reduce.2.cloned.1.call-start = ((), (), s32[]{:S(2)}) async-start(), calls=%async_computation.2 | async-start | bytes 4718592 | tf_op jit(solution)/shard_map/psum | solution.py:175
  154.1 1.7 copy-start.1
Sparse Core Ops, SparseCore 0:
  45.0 109.0 all-reduce.1

commit v2 on v1

--- a/solution.py
+++ b/solution.py
@@ -119,6 +119,95 @@
                 )
 
 
+def total_kernel(stages, chunks, part_ref, out_ref, acc_ref, inbox_ref, send_sem, recv_sem):
+    me = lax.axis_index("sec")
+    rows = part_ref.shape[0] // chunks
+    bit = [(me // (1 << s)) % 2 for s in range(stages)]
+    peer = [me + (1 << s) * (1 - 2 * bit[s]) for s in range(stages)]
+    barrier = pltpu.get_barrier_semaphore()
+    for s in range(stages):
+        pl.semaphore_signal(
+            barrier, inc=1, device_id={"sec": peer[s]}, device_id_type=pl.DeviceIdType.MESH
+        )
+    pl.semaphore_wait(barrier, stages)
+
+    base = [[None] * (stages + 1) for _ in range(chunks)]
+    for c in range(chunks):
+        base[c][0] = c * rows
+        for s in range(stages):
+            base[c][s + 1] = base[c][s] + bit[s] * (rows >> (s + 1))
+
+    def window(c, s, flip):
+        size = rows >> (s + 1)
+        side = 1 - bit[s] if flip else bit[s]
+        return pl.ds(pl.multiple_of(base[c][s] + side * size, 8), size)
+
+    def box(c, s):
+        return pl.ds(c * rows + rows - (rows >> s), rows >> (s + 1))
+
+    def make(c, t):
+        if t < stages:
+            source = part_ref if t == 0 else acc_ref
+            src = source.at[window(c, t, True), :]
+            dst = inbox_ref.at[box(c, t), :]
+            s = t
+        else:
+            s = 2 * stages - 1 - t
+            src = out_ref.at[window(c, s, False), :]
+            dst = out_ref.at[window(c, s, False), :]
+        return pltpu.make_async_remote_copy(
+            src_ref=src,
+            dst_ref=dst,
+            send_sem=send_sem.at[c, t],
+            recv_sem=recv_sem.at[c, t],
+            device_id={"sec": peer[s]},
+            device_id_type=pl.DeviceIdType.MESH,
+        )
+
+    copies = {}
+    for step in range(2 * stages + chunks):
+        for c in range(chunks):
+            t = step - c
+            if t < 0 or t > 2 * stages:
+                continue
+            if t > 0:
+                copies[c, t - 1].wait()
+                if t <= stages:
+                    mine = window(c, t - 1, False)
+                    source = part_ref if t == 1 else acc_ref
+                    result = out_ref if t == stages else acc_ref
+                    result[mine, :] = source[mine, :] + inbox_ref[box(c, t - 1), :]
+            if t < 2 * stages:
+                copies[c, t] = make(c, t)
+                copies[c, t].start()
+
+
+def total_over_sec(part, owners):
+    stages = owners.bit_length() - 1
+    grain = 8 * owners
+    chunks = 4 if part.shape[0] % (4 * grain) == 0 else 1
+    rows = -(-part.shape[0] // grain) * grain
+    padded = jnp.pad(part, ((0, rows - part.shape[0]), (0, 0)))
+    vmem = pl.BlockSpec(memory_space=pltpu.VMEM)
+    total = pl.pallas_call(
+        lambda *refs: total_kernel(stages, chunks, *refs),
+        out_shape=jax.ShapeDtypeStruct((rows, B), F32),
+        in_specs=[vmem],
+        out_specs=vmem,
+        scratch_shapes=[
+            pltpu.VMEM((rows, B), F32),
+            pltpu.VMEM((rows, B), F32),
+            pltpu.SemaphoreType.DMA((chunks, 2 * stages)),
+            pltpu.SemaphoreType.DMA((chunks, 2 * stages)),
+        ],
+        compiler_params=pltpu.CompilerParams(
+            collective_id=0, has_side_effects=True, vmem_limit_bytes=40 << 20
+        ),
+        name="total_over_sec",
+    )(padded)
+    return total[: part.shape[0]]
+
+
 def products(rows, corner):
     nb = corner.shape[1] // B
     _, total = starts(nb)
@@ -172,7 +261,7 @@
         tiled=True,
     )
     product, gram_part = products(arrived.reshape(owners * capacity, feature_len), corner)
-    gram = lax.psum(gram_part, "sec")
+    gram = total_over_sec(gram_part, owners)
     returned = lax.all_to_all(
         product.reshape(owners, capacity, feature_len),
         "sec",

time: 227 us -> 159 us (0.70)
  waiting for transfers between devices: 113 us -> 0.01 us
  Pallas kernels: 68.1 us -> 123 us
  between operations: 13.5 us -> 0.1 us
  local copies, waits for them, and re-layouts: 5.47 us -> 9.31 us
    psum x1 -> x0, waiting for transfers between devices: 84.3 us -> none  [per_device(): gram = lax.psum(gram_part, 'sec')]
    pallas_call x0 -> x1, Pallas kernels: none -> 56 us  [total_over_sec(): pl.pallas_call(lambda *refs: total_kernel(stages, chunks, *refs), out_sha...]
    all_to_all x1, waiting for transfers between devices: 27.6 us -> 0.01 us  [per_device(): lax.all_to_all(product.reshape(owners, capacity, feature_len), 'sec', spl...]
    unnamed x6 -> x10, local copies, waits for them, and re-layouts: 1.67 us -> 4.05 us
  transfers between devices with their start and end apart: 2 -> 1, of which waited for: 2 -> 0; matrix products, arithmetic and copies ran while one was open for 0% -> 0% of each run, Pallas kernels for 0% -> 35%
where the time goes in v2:
time: 159 us
  Pallas kernels  123 us (77%)
  blocking collectives  21.7 us (14%)
  local copies, waits for them, and re-layouts  9.31 us (6%)
  starting transfers between devices  4.1 us (3%)
    pallas_call x1, Pallas kernels, solve_rows(): pl.pallas_call(lambda *refs: solve_kernel(nb, factor, *refs), out_shape=j...  64.1 us
    pallas_call x1, Pallas kernels, total_over_sec(): pl.pallas_call(lambda *refs: total_kernel(stages, chunks, *refs), out_sha...  56 us
    all_to_all x1, blocking collectives, per_device(): lax.all_to_all(packed.reshape(owners, capacity, feature_len), 'sec', spli...  21.7 us
    all_to_all x1, starting transfers between devices, per_device(): lax.all_to_all(product.reshape(owners, capacity, feature_len), 'sec', spl...  4.1 us
    unnamed x10, local copies, waits for them, and re-layouts  4.05 us
  transfers between devices with their start and end apart: 1, of which 0 were waited for; matrix products, arithmetic and copies ran while one was open for 0% of the time, Pallas kernels for 35%

profile of v2, /device:TPU:0, one launch (start us, length us, event | category | flops | bytes accessed | tf_op | source)
XLA Modules:
  0.0 159.1 jit_solution(4577963285269758084)
XLA Ops:
  0.0 0.0 copy-start
  0.0 0.0 copy-start.3
  0.0 0.8 fusion.5
  0.8 0.0 copy-done
  0.8 1.3 gather_fusion
  2.1 0.1 fusion.2
  2.2 0.2 reduce_window_sum.11
  2.4 0.2 select_reduce_fusion
  2.6 1.7 %scatter_custom_fusion = bf16[256,1024]{1,0:T(8,128)(2,1)S(1)} fusion(s32[128]{0:T(128)S(1)} %fusion.8, bf16[128,1024]{1,0:T(8,128)(2,1)} %param.5, bf16[]{:T(256)} %constant.4.clone.1), kind=kCustom, calls=%fused_computation.3 | custom fusion | bytes 524800 | tf_op jit(solution)/shard_map/scatter | solution.py:254
  4.3 21.7 %all_to_all.10 = bf16[16,16,1024]{2,1,0:T(8,128)(2,1)S(1)} all-to-all(bf16[16,16,1024]{2,1,0:T(8,128)(2,1)S(1)} %bitcast.10), channel_id=1, replica_groups=mesh['runs'=2,'sec'=16] {'sec'}, dimensions={0} | all-to-all | bytes 1048576 | tf_op jit(solution)/shard_map/all_to_all | solution.py:256
  26.0 0.0 copy-done.3
  26.0 2.6 %products.1 = (f32[256,1024]{1,0:T(8,128)}, f32[4608,128]{1,0:T(8,128)S(1)}) custom-call(bf16[256,1024]{1,0:T(8,128)(2,1)S(1)} %bitcast.8, bf16[1024,1024]{1,0:T(8,128)(2,1)S(1)} %copy-done.3), custom_call_target="tpu_custom_call" | custom-call | tf_op jit(solution)/shard_map/products/pallas_call | solution.py:215
  28.6 0.0 copy-start.1
  28.6 1.4 copy-done.1
  30.0 4.1 %all-to-all-start.1 = ((f32[16,16,1024]{2,1,0:T(8,128)}), f32[16,16,1024]{2,1,0:T(8,128)S(1)}, u32[]{:S(2)}, u32[]{:S(2)}) async-start(f32[16,16,1024]{2,1,0:T(8,128)} %bitcast.4), calls=%async_computation.1 | async-start | bytes 2097152 | tf_op jit(solution)/shard_map/all_to_all | solution.py:265
  34.1 0.0 copy-start.2
  34.1 1.7 %copy-done.2 = f32[4608,128]{1,0:T(8,128)S(1)} copy-done((f32[4608,128]{1,0:T(8,128)S(1)}, f32[4608,128]{1,0:T(8,128)}, u32[]{:S(2)}) %copy-start.2) | copy-done | bytes 2359320
  35.8 56.0 %total_over_sec.1.refs_0_ = f32[4608,128]{1,0:T(8,128)S(1)} custom-call(f32[4608,128]{1,0:T(8,128)S(1)} %copy-done.2), custom_call_target="tpu_custom_call" | custom-call | tf_op jit(solution)/shard_map/total_over_sec/pallas_call | solution.py:192
  91.8 0.0 all-to-all-done.1
  91.8 0.0 copy-start.4
  91.8 1.0 copy-done.4
  92.8 2.3 %gather_fusion.1 = f32[128,1024]{1,0:T(8,128)S(1)} fusion(f32[256,1024]{1,0:T(8,128)} %bitcast.9, s32[1024]{0:T(1024)S(1)} %pad_clamp_fusion), kind=kCustom, calls=%fused_computation.1 | custom fusion | bytes 1049088 | tf_op jit(solution)/shard_map/gather | solution.py:272
  95.0 64.1 %solve_rows.1 = f32[128,1024]{1,0:T(8,128)} custom-call(f32[4608,128]{1,0:T(8,128)S(1)} %total_over_sec.1.refs_0_, f32[128,1024]{1,0:T(8,128)S(1)} %gather_fusion.1), custom_call_target="tpu_custom_call" | custom-call | tf_op jit(solution)/shard_map/solve_rows/pallas_call | solution.py:231
  (2 shorter events, 0.0 us)
Async XLA Ops:
  0.0 0.8 copy-start
  0.0 26.0 %copy-start.3 = (bf16[1024,1024]{1,0:T(8,128)(2,1)S(1)}, bf16[1024,1024]{1,0:T(8,128)(2,1)}, u32[]{:S(2)}) copy-start(bf16[1024,1024]{1,0:T(8,128)(2,1)} %refs_1_.1) | copy-start | bytes 6291460
  28.6 1.4 copy-start.1
  30.0 61.8 %all-to-all-start.1 = ((f32[16,16,1024]{2,1,0:T(8,128)}), f32[16,16,1024]{2,1,0:T(8,128)S(1)}, u32[]{:S(2)}, u32[]{:S(2)}) async-start(f32[16,16,1024]{2,1,0:T(8,128)} %bitcast.4), calls=%async_computation.1 | async-start | bytes 2097152 | tf_op jit(solution)/shard_map/all_to_all | solution.py:265
  34.1 1.7 %copy-start.2 = (f32[4608,128]{1,0:T(8,128)S(1)}, f32[4608,128]{1,0:T(8,128)}, u32[]{:S(2)}) copy-start(f32[4608,128]{1,0:T(8,128)} %copy-done.1) | copy-start | bytes 7077892
  91.8 1.0 copy-start.4

commit v3 on v2

--- a/solution.py
+++ b/solution.py
@@ -8,7 +8,7 @@
 from jax.sharding import PartitionSpec as P
 
 B = 128
-S = 8
+S = 32
 F32 = jnp.float32
 BF16 = jnp.bfloat16
 

time: 159 us -> 137 us (0.86)
  Pallas kernels: 123 us -> 101 us
    pallas_call x1, Pallas kernels: 64.1 us -> 42 us  [solve_rows(): pl.pallas_call(lambda *refs: solve_kernel(nb, factor, *refs), out_shape=j...]
  transfers between devices with their start and end apart: 1 -> 1, of which waited for: 0 -> 0; matrix products, arithmetic and copies ran while one was open for 0% -> 0% of each run, Pallas kernels for 35% -> 41%
where the time goes in v3:
time: 137 us
  Pallas kernels  101 us (74%)
  blocking collectives  21.7 us (16%)
  local copies, waits for them, and re-layouts  9.31 us (7%)
  starting transfers between devices  4.11 us (3%)
    pallas_call x1, Pallas kernels, total_over_sec(): pl.pallas_call(lambda *refs: total_kernel(stages, chunks, *refs), out_sha...  56 us
    pallas_call x1, Pallas kernels, solve_rows(): pl.pallas_call(lambda *refs: solve_kernel(nb, factor, *refs), out_shape=j...  42 us
    all_to_all x1, blocking collectives, per_device(): lax.all_to_all(packed.reshape(owners, capacity, feature_len), 'sec', spli...  21.7 us
    all_to_all x1, starting transfers between devices, per_device(): lax.all_to_all(product.reshape(owners, capacity, feature_len), 'sec', spl...  4.11 us
    unnamed x10, local copies, waits for them, and re-layouts  4.05 us
  transfers between devices with their start and end apart: 1, of which 0 were waited for; matrix products, arithmetic and copies ran while one was open for 0% of the time, Pallas kernels for 41%

profile of v3, /device:TPU:0, one launch (start us, length us, event | category | flops | bytes accessed | tf_op | source)
XLA Modules:
  0.0 137.0 jit_solution(18423941844693813824)
XLA Ops:
  0.0 0.0 copy-start
  0.0 0.0 copy-start.3
  0.0 0.8 fusion.5
  0.8 0.0 copy-done
  0.8 1.3 gather_fusion
  2.1 0.1 fusion.2
  2.2 0.2 reduce_window_sum.11
  2.4 0.2 select_reduce_fusion
  2.6 1.7 %scatter_custom_fusion = bf16[256,1024]{1,0:T(8,128)(2,1)S(1)} fusion(s32[128]{0:T(128)S(1)} %fusion.8, bf16[128,1024]{1,0:T(8,128)(2,1)} %param.5, bf16[]{:T(256)} %constant.4.clone.1), kind=kCustom, calls=%fused_computation.3 | custom fusion | bytes 524800 | tf_op jit(solution)/shard_map/scatter | solution.py:254
  4.3 21.7 %all_to_all.10 = bf16[16,16,1024]{2,1,0:T(8,128)(2,1)S(1)} all-to-all(bf16[16,16,1024]{2,1,0:T(8,128)(2,1)S(1)} %bitcast.10), channel_id=1, replica_groups=mesh['runs'=2,'sec'=16] {'sec'}, dimensions={0} | all-to-all | bytes 1048576 | tf_op jit(solution)/shard_map/all_to_all | solution.py:256
  26.0 0.0 copy-done.3
  26.0 2.6 %products.1 = (f32[256,1024]{1,0:T(8,128)}, f32[4608,128]{1,0:T(8,128)S(1)}) custom-call(bf16[256,1024]{1,0:T(8,128)(2,1)S(1)} %bitcast.8, bf16[1024,1024]{1,0:T(8,128)(2,1)S(1)} %copy-done.3), custom_call_target="tpu_custom_call" | custom-call | tf_op jit(solution)/shard_map/products/pallas_call | solution.py:215
  28.6 0.0 copy-start.1
  28.6 1.4 %copy-done.1 = f32[4608,128]{1,0:T(8,128)} copy-done((f32[4608,128]{1,0:T(8,128)}, f32[4608,128]{1,0:T(8,128)S(1)}, u32[]{:S(2)}) %copy-start.1) | copy-done | bytes 2359320
  30.0 4.1 %all-to-all-start.1 = ((f32[16,16,1024]{2,1,0:T(8,128)}), f32[16,16,1024]{2,1,0:T(8,128)S(1)}, u32[]{:S(2)}, u32[]{:S(2)}) async-start(f32[16,16,1024]{2,1,0:T(8,128)} %bitcast.4), calls=%async_computation.1 | async-start | bytes 2097152 | tf_op jit(solution)/shard_map/all_to_all | solution.py:265
  34.1 0.0 copy-start.2
  34.2 1.7 %copy-done.2 = f32[4608,128]{1,0:T(8,128)S(1)} copy-done((f32[4608,128]{1,0:T(8,128)S(1)}, f32[4608,128]{1,0:T(8,128)}, u32[]{:S(2)}) %copy-start.2) | copy-done | bytes 2359320
  35.8 56.0 %total_over_sec.1.refs_0_ = f32[4608,128]{1,0:T(8,128)S(1)} custom-call(f32[4608,128]{1,0:T(8,128)S(1)} %copy-done.2), custom_call_target="tpu_custom_call" | custom-call | tf_op jit(solution)/shard_map/total_over_sec/pallas_call | solution.py:192
  91.8 0.0 all-to-all-done.1
  91.8 0.0 copy-start.4
  91.8 1.0 copy-done.4
  92.8 2.3 %gather_fusion.1 = f32[128,1024]{1,0:T(8,128)S(1)} fusion(f32[256,1024]{1,0:T(8,128)} %bitcast.9, s32[1024]{0:T(1024)S(1)} %pad_clamp_fusion), kind=kCustom, calls=%fused_computation.1 | custom fusion | bytes 1049088 | tf_op jit(solution)/shard_map/gather | solution.py:272
  95.0 42.0 %solve_rows.1 = f32[128,1024]{1,0:T(8,128)} custom-call(f32[4608,128]{1,0:T(8,128)S(1)} %total_over_sec.1.refs_0_, f32[128,1024]{1,0:T(8,128)S(1)} %gather_fusion.1), custom_call_target="tpu_custom_call" | custom-call | tf_op jit(solution)/shard_map/solve_rows/pallas_call | solution.py:231
  (2 shorter events, 0.0 us)
Async XLA Ops:
  0.0 0.8 copy-start
  0.0 26.0 %copy-start.3 = (bf16[1024,1024]{1,0:T(8,128)(2,1)S(1)}, bf16[1024,1024]{1,0:T(8,128)(2,1)}, u32[]{:S(2)}) copy-start(bf16[1024,1024]{1,0:T(8,128)(2,1)} %refs_1_.1) | copy-start | bytes 6291460
  28.6 1.4 %copy-start.1 = (f32[4608,128]{1,0:T(8,128)}, f32[4608,128]{1,0:T(8,128)S(1)}, u32[]{:S(2)}) copy-start(f32[4608,128]{1,0:T(8,128)S(1)} %get-tuple-element.7.refs_0_) | copy-start | bytes 7077892
  30.0 61.8 %all-to-all-start.1 = ((f32[16,16,1024]{2,1,0:T(8,128)}), f32[16,16,1024]{2,1,0:T(8,128)S(1)}, u32[]{:S(2)}, u32[]{:S(2)}) async-start(f32[16,16,1024]{2,1,0:T(8,128)} %bitcast.4), calls=%async_computation.1 | async-start | bytes 2097152 | tf_op jit(solution)/shard_map/all_to_all | solution.py:265
  34.1 1.7 %copy-start.2 = (f32[4608,128]{1,0:T(8,128)S(1)}, f32[4608,128]{1,0:T(8,128)}, u32[]{:S(2)}) copy-start(f32[4608,128]{1,0:T(8,128)} %copy-done.1) | copy-start | bytes 7077892
  91.8 1.0 copy-start.4

commit v4 on v3

--- a/solution.py
+++ b/solution.py
@@ -84,39 +84,58 @@
     lax.fori_loop(0, B // S, step, 0)
 
 
-def solve_kernel(nb, factor, gram_ref, home_ref, out_ref, a_ref, t_ref):
-    offs, total = starts(nb)
-    rows = home_ref.shape[0]
-    a_ref[...] = gram_ref[...]
-    out_ref[...] = home_ref[...]
+def factor_kernel(nb, gram_ref, low_ref, t_ref):
+    offs, _ = starts(nb)
+    low_ref[...] = gram_ref[...]
     eye = (
         lax.broadcasted_iota(jnp.int32, (B, B), 0) == lax.broadcasted_iota(jnp.int32, (B, B), 1)
     ).astype(F32)
     for k in range(nb):
-        t_ref[:, :B] = a_ref[pl.ds(offs[k], B), :]
+        t_ref[:, :B] = low_ref[pl.ds(offs[k], B), :]
         t_ref[:, B:] = eye
         factor_block(t_ref)
-        ih, il = split2(t_ref[:, B:])
-        inv = jnp.concatenate([ih, il, ih], axis=1)
+        low_ref[pl.ds(offs[k], B), :] = t_ref[:, B:]
         below = (nb - k - 1) * B
-        x = out_ref[:, k * B : (k + 1) * B]
         if below:
-            x = jnp.concatenate([a_ref[pl.ds(offs[k] + B, below), :], x], axis=0)
-        xh, xl = split2(x)
-        panel = dot(jnp.concatenate([xh, xh, xl], axis=1), inv, ((1,), (1,)))
-        out_ref[:, k * B : (k + 1) * B] = panel[below:, :] * factor
-        if below:
+            ih, il = split2(t_ref[:, B:])
+            xh, xl = split2(low_ref[pl.ds(offs[k] + B, below), :])
+            panel = dot(
+                jnp.concatenate([xh, xh, xl], axis=1),
+                jnp.concatenate([ih, il, ih], axis=1),
+                ((1,), (1,)),
+            )
+            low_ref[pl.ds(offs[k] + B, below), :] = panel
             ph, plo = split2(panel)
             left = jnp.concatenate([ph, ph, plo], axis=1)
             right = jnp.concatenate([ph, plo, ph], axis=1)
             for j in range(k + 1, nb):
                 at = (j - k - 1) * B
                 change = dot(left[at:, :], right[at : at + B, :], ((1,), (1,)))
-                size = (nb - j) * B
-                a_ref[pl.ds(offs[j], size), :] = a_ref[pl.ds(offs[j], size), :] - change[:size, :]
-                out_ref[:, j * B : (j + 1) * B] = (
-                    out_ref[:, j * B : (j + 1) * B] - change[size:, :]
-                )
+                here = pl.ds(offs[j], (nb - j) * B)
+                low_ref[here, :] = low_ref[here, :] - change
+
+
+def apply_kernel(nb, factor, low_ref, home_ref, out_ref):
+    offs, _ = starts(nb)
+    rest = home_ref[...]
+    for k in range(nb):
+        ih, il = split2(low_ref[pl.ds(offs[k], B), :])
+        xh, xl = split2(rest[:, :B])
+        x = dot(
+            jnp.concatenate([xh, xh, xl], axis=1),
+            jnp.concatenate([ih, il, ih], axis=1),
+            ((1,), (1,)),
+        )
+        out_ref[:, k * B : (k + 1) * B] = x * factor
+        below = (nb - k - 1) * B
+        if below:
+            ph, plo = split2(low_ref[pl.ds(offs[k] + B, below), :])
+            xh, xl = split2(x)
+            rest = rest[:, B:] - dot(
+                jnp.concatenate([xh, xh, xl], axis=1),
+                jnp.concatenate([ph, plo, ph], axis=1),
+                ((1,), (1,)),
+            )
 
 
 def total_kernel(stages, chunks, part_ref, out_ref, acc_ref, inbox_ref, send_sem, recv_sem):
@@ -225,18 +244,34 @@
     )(rows, corner)
 
 
-def solve_rows(gram, home, factor):
+def factor_gram(gram):
+    nb = int((2 * gram.shape[0] // B) ** 0.5)
+    vmem = pl.BlockSpec(memory_space=pltpu.VMEM)
+    return pl.pallas_call(
+        lambda *refs: factor_kernel(nb, *refs),
+        out_shape=jax.ShapeDtypeStruct(gram.shape, F32),
+        in_specs=[vmem],
+        out_specs=vmem,
+        scratch_shapes=[pltpu.VMEM((B, 2 * B), F32)],
+        compiler_params=pltpu.CompilerParams(vmem_limit_bytes=40 << 20),
+        cost_estimate=pl.CostEstimate(
+            flops=30_000_000_000, bytes_accessed=80_000_000, transcendentals=0
+        ),
+        name="factor_gram",
+    )(gram)
+
+
+def apply_factor(low, home, factor):
     nb = home.shape[1] // B
     vmem = pl.BlockSpec(memory_space=pltpu.VMEM)
     return pl.pallas_call(
-        lambda *refs: solve_kernel(nb, factor, *refs),
+        lambda *refs: apply_kernel(nb, factor, *refs),
         out_shape=jax.ShapeDtypeStruct(home.shape, F32),
         in_specs=[vmem, vmem],
         out_specs=vmem,
-        scratch_shapes=[pltpu.VMEM(gram.shape, F32), pltpu.VMEM((B, 2 * B), F32)],
-        compiler_params=pltpu.CompilerParams(vmem_limit_bytes=48 << 20),
-        name="solve_rows",
-    )(gram, home)
+        compiler_params=pltpu.CompilerParams(vmem_limit_bytes=40 << 20),
+        name="apply_factor",
+    )(low, home)
 
 
 def per_device(edge_rows, corner, joining, charge_left, charge_right):
@@ -262,6 +297,7 @@
     )
     product, gram_part = products(arrived.reshape(owners * capacity, feature_len), corner)
     gram = total_over_sec(gram_part, owners)
+    gram, product = lax.optimization_barrier((gram, product))
     returned = lax.all_to_all(
         product.reshape(owners, capacity, feature_len),
         "sec",
@@ -270,7 +306,7 @@
         tiled=True,
     )
     home_rows = returned.reshape(owners * capacity, feature_len)[slot_index]
-    return solve_rows(gram, home_rows, factor)
+    return apply_factor(factor_gram(gram), home_rows, factor)
 
 
 def solution(mesh):

time: 137 us -> 127 us (0.927)
  blocking collectives: 21.7 us -> 0 us
  waiting for transfers between devices: 0.01 us -> 14.5 us
  Pallas kernels: 101 us -> 90.3 us
  starting transfers between devices: 4.11 us -> 12.4 us
    all_to_all x1 -> x0, blocking collectives: 21.7 us -> none  [per_device(): lax.all_to_all(packed.reshape(owners, capacity, feature_len), 'sec', spli...]
    all_to_all x0 -> x1, waiting for transfers between devices: none -> 14.5 us  [per_device(): lax.all_to_all(packed.reshape(owners, capacity, feature_len), 'sec', spli...]
    pallas_call x1, Pallas kernels: 56 us -> 44.4 us  [total_over_sec(): pl.pallas_call(lambda *refs: total_kernel(stages, chunks, *refs), out_sha...]
    all_to_all x0 -> x1, starting transfers between devices: none -> 7.39 us  [per_device(): lax.all_to_all(packed.reshape(owners, capacity, feature_len), 'sec', spli...]
    unnamed x10 -> x12, local copies, waits for them, and re-layouts: 4.05 us -> 2.4 us
    pallas_call x1 -> x2, Pallas kernels: 42 us -> 43.3 us  [the longest x1 40.2 us: factor_gram(): pl.pallas_call(lambda *refs: factor_kernel(nb, *refs), out_shape=jax.Shap...]
  transfers between devices with their start and end apart: 1 -> 2, of which waited for: 0 -> 1; matrix products, arithmetic and copies ran while one was open for 0% -> 0% of each run, Pallas kernels for 41% -> 32%
where the time goes in v4:
time: 127 us
  Pallas kernels  90.3 us (71%)
  waiting for transfers between devices  14.5 us (11%)
  starting transfers between devices  12.4 us (10%)
  local copies, waits for them, and re-layouts  8.46 us (7%)
  other arithmetic  1.27 us (1%)
    pallas_call x1, Pallas kernels, total_over_sec(): pl.pallas_call(lambda *refs: total_kernel(stages, chunks, *refs), out_sha...  44.4 us
    pallas_call x1, Pallas kernels, factor_gram(): pl.pallas_call(lambda *refs: factor_kernel(nb, *refs), out_shape=jax.Shap...  40.2 us
    all_to_all x1, waiting for transfers between devices, per_device(): lax.all_to_all(packed.reshape(owners, capacity, feature_len), 'sec', spli...  14.5 us
    all_to_all x1, starting transfers between devices, per_device(): lax.all_to_all(packed.reshape(owners, capacity, feature_len), 'sec', spli...  7.39 us
    all_to_all x1, starting transfers between devices, per_device(): lax.all_to_all(product.reshape(owners, capacity, feature_len), 'sec', spl...  5.01 us
    pallas_call x1, Pallas kernels, apply_factor(): pl.pallas_call(lambda *refs: apply_kernel(nb, factor, *refs), out_shape=j...  3.11 us
    pallas_call x1, Pallas kernels, products(): pl.pallas_call(lambda *refs: product_kernel(nb, *refs), out_shape=(jax.Sh...  2.63 us
  transfers between devices with their start and end apart: 2, of which 1 were waited for; matrix products, arithmetic and copies ran while one was open for 0% of the time, Pallas kernels for 32%

profile of v4, /device:TPU:0, one launch (start us, length us, event | category | flops | bytes accessed | tf_op | source)
XLA Modules:
  0.0 127.0 jit_solution(13139519960824110864)
XLA Ops:
  0.0 0.0 copy-start
  0.0 0.0 copy-start.3
  0.0 0.8 fusion.5
  0.8 0.0 copy-done
  0.8 1.3 gather_fusion
  2.1 0.1 fusion.2
  2.2 0.2 reduce_window_sum.11
  2.4 0.2 select_reduce_fusion
  2.6 2.4 %scatter_custom_fusion = bf16[256,1024]{1,0:T(8,128)(2,1)} fusion(s32[128]{0:T(128)S(1)} %fusion.8, bf16[128,1024]{1,0:T(8,128)(2,1)} %param.5, bf16[]{:T(256)} %constant.4.clone.1), kind=kCustom, calls=%fused_computation.3 | custom fusion | bytes 524800 | tf_op jit(solution)/shard_map/scatter | solution.py:289
  4.9 7.4 %all-to-all-start = ((bf16[16,16,1024]{2,1,0:T(8,128)(2,1)}), bf16[16,16,1024]{2,1,0:T(8,128)(2,1)S(1)}, u32[]{:S(2)}, u32[]{:S(2)}) async-start(bf16[16,16,1024]{2,1,0:T(8,128)(2,1)} %bitcast.2), calls=%async_computation | async-start | bytes 1048576 | tf_op jit(solution)/shard_map/all_to_all | solution.py:291
  12.3 14.5 %all-to-all-done = bf16[16,16,1024]{2,1,0:T(8,128)(2,1)S(1)} async-done(((bf16[16,16,1024]{2,1,0:T(8,128)(2,1)}), bf16[16,16,1024]{2,1,0:T(8,128)(2,1)S(1)}, u32[]{:S(2)}, u32[]{:S(2)}) %all-to-all-start) | async-done | bytes 524320 | tf_op jit(solution)/shard_map/all_to_all | solution.py:291
  26.8 0.0 copy-done.3
  26.8 2.6 %products.1 = (f32[256,1024]{1,0:T(8,128)S(1)}, f32[4608,128]{1,0:T(8,128)S(1)}) custom-call(bf16[256,1024]{1,0:T(8,128)(2,1)S(1)} %bitcast.8, bf16[1024,1024]{1,0:T(8,128)(2,1)S(1)} %copy-done.3), custom_call_target="tpu_custom_call" | custom-call | tf_op jit(solution)/shard_map/products/pallas_call | solution.py:234
  29.4 0.0 copy-start.4
  29.5 44.4 %total_over_sec.1.refs_0_ = f32[4608,128]{1,0:T(8,128)S(1)} custom-call(f32[4608,128]{1,0:T(8,128)S(1)} %get-tuple-element.9.refs_0_), custom_call_target="tpu_custom_call" | custom-call | tf_op jit(solution)/shard_map/total_over_sec/pallas_call | solution.py:211
  73.9 0.0 copy-done.4
  73.9 5.0 %all-to-all-start.1 = ((f32[16,16,1024]{2,1,0:T(8,128)}), f32[16,16,1024]{2,1,0:T(8,128)S(1)}, u32[]{:S(2)}, u32[]{:S(2)}) async-start(f32[16,16,1024]{2,1,0:T(8,128)} %bitcast.9), calls=%async_computation.1 | async-start | bytes 2097152 | tf_op jit(solution)/shard_map/all_to_all | solution.py:301
  78.9 40.2 %factor_gram.1.refs_0_ = f32[4608,128]{1,0:T(8,128)S(1)} custom-call(f32[4608,128]{1,0:T(8,128)S(1)} %total_over_sec.1.refs_0_), custom_call_target="tpu_custom_call" | custom-call | flops 30000001024 | bytes 80000000 | tf_op jit(solution)/shard_map/factor_gram/pallas_call | solution.py:250
  119.1 0.0 copy-start.1
  119.1 1.4 %copy-done.1 = f32[4608,128]{1,0:T(8,128)} copy-done((f32[4608,128]{1,0:T(8,128)}, f32[4608,128]{1,0:T(8,128)S(1)}, u32[]{:S(2)}) %copy-start.1) | copy-done | bytes 2359320
  120.5 0.0 all-to-all-done.1
  120.5 0.0 copy-start.5
  120.5 1.0 copy-done.5
  121.5 0.0 copy-start.2
  121.5 2.4 %gather_fusion.1 = f32[128,1024]{1,0:T(8,128)S(1)} fusion(f32[256,1024]{1,0:T(8,128)} %bitcast.10, s32[1024]{0:T(1024)S(1)} %pad_clamp_fusion), kind=kCustom, calls=%fused_computation.1 | custom fusion | bytes 1049088 | tf_op jit(solution)/shard_map/gather | solution.py:308
  123.9 0.0 copy-done.2
  123.9 3.1 %apply_factor.1 = f32[128,1024]{1,0:T(8,128)} custom-call(f32[4608,128]{1,0:T(8,128)S(1)} %copy-done.2, f32[128,1024]{1,0:T(8,128)S(1)} %gather_fusion.1), custom_call_target="tpu_custom_call" | custom-call | tf_op jit(solution)/shard_map/apply_factor/pallas_call | solution.py:267
  (2 shorter events, 0.0 us)
Async XLA Ops:
  0.0 0.8 copy-start
  0.0 26.8 %copy-start.3 = (bf16[1024,1024]{1,0:T(8,128)(2,1)S(1)}, bf16[1024,1024]{1,0:T(8,128)(2,1)}, u32[]{:S(2)}) copy-start(bf16[1024,1024]{1,0:T(8,128)(2,1)} %refs_1_.1) | copy-start | bytes 6291460
  4.9 21.9 %all-to-all-start = ((bf16[16,16,1024]{2,1,0:T(8,128)(2,1)}), bf16[16,16,1024]{2,1,0:T(8,128)(2,1)S(1)}, u32[]{:S(2)}, u32[]{:S(2)}) async-start(bf16[16,16,1024]{2,1,0:T(8,128)(2,1)} %bitcast.2), calls=%async_computation | async-start | bytes 1048576 | tf_op jit(solution)/shard_map/all_to_all | solution.py:291
  29.4 44.4 %copy-start.4 = (f32[256,1024]{1,0:T(8,128)}, f32[256,1024]{1,0:T(8,128)S(1)}, u32[]{:S(2)}) copy-start(f32[256,1024]{1,0:T(8,128)S(1)} %get-tuple-element.12) | copy-start | bytes 3145732
  73.9 46.6 %all-to-all-start.1 = ((f32[16,16,1024]{2,1,0:T(8,128)}), f32[16,16,1024]{2,1,0:T(8,128)S(1)}, u32[]{:S(2)}, u32[]{:S(2)}) async-start(f32[16,16,1024]{2,1,0:T(8,128)} %bitcast.9), calls=%async_computation.1 | async-start | bytes 2097152 | tf_op jit(solution)/shard_map/all_to_all | solution.py:301
  119.1 1.4 %copy-start.1 = (f32[4608,128]{1,0:T(8,128)}, f32[4608,128]{1,0:T(8,128)S(1)}, u32[]{:S(2)}) copy-start(f32[4608,128]{1,0:T(8,128)S(1)} %factor_gram.1.refs_0_) | copy-start | bytes 7077892
  120.5 1.0 copy-start.5
  121.5 2.4 %copy-start.2 = (f32[4608,128]{1,0:T(8,128)S(1)}, f32[4608,128]{1,0:T(8,128)}, u32[]{:S(2)}) copy-start(f32[4608,128]{1,0:T(8,128)} %copy-done.1) | copy-start | bytes 7077892

commit v5 on v4

--- a/solution.py
+++ b/solution.py
@@ -115,9 +115,20 @@
                 low_ref[here, :] = low_ref[here, :] - change
 
 
-def apply_kernel(nb, factor, low_ref, home_ref, out_ref):
+def hot(index, count):
+    lane = lax.broadcasted_iota(jnp.int32, (index.shape[0], count), 1)
+    return (lane == index).astype(F32)
+
+
+def apply_kernel(nb, factor, low_ref, back_ref, slot_ref, out_ref):
     offs, _ = starts(nb)
-    rest = home_ref[...]
+    back = back_ref[...]
+    pick = hot(slot_ref[...], back.shape[0]).astype(BF16)
+    hi = back.astype(BF16)
+    mid, lo = split2(back - hi.astype(F32))
+    rest = dot(pick, hi, ((1,), (0,))) + (
+        dot(pick, mid, ((1,), (0,))) + dot(pick, lo, ((1,), (0,)))
+    )
     for k in range(nb):
         ih, il = split2(low_ref[pl.ds(offs[k], B), :])
         xh, xl = split2(rest[:, :B])
@@ -204,7 +215,7 @@
 def total_over_sec(part, owners):
     stages = owners.bit_length() - 1
     grain = 8 * owners
-    chunks = 4 if part.shape[0] % (4 * grain) == 0 else 1
+    chunks = 6 if part.shape[0] % (6 * grain) == 0 else 1
     rows = -(-part.shape[0] // grain) * grain
     padded = jnp.pad(part, ((0, rows - part.shape[0]), (0, 0)))
     vmem = pl.BlockSpec(memory_space=pltpu.VMEM)
@@ -220,7 +231,7 @@
             pltpu.SemaphoreType.DMA((chunks, 2 * stages)),
         ],
         compiler_params=pltpu.CompilerParams(
-            collective_id=0, has_side_effects=True, vmem_limit_bytes=40 << 20
+            collective_id=0, has_side_effects=True, vmem_limit_bytes=20 << 20
         ),
         name="total_over_sec",
     )(padded)
@@ -239,7 +250,7 @@
         ),
         in_specs=[vmem, vmem],
         out_specs=(vmem, vmem),
-        compiler_params=pltpu.CompilerParams(vmem_limit_bytes=48 << 20),
+        compiler_params=pltpu.CompilerParams(vmem_limit_bytes=20 << 20),
         name="products",
     )(rows, corner)
 
@@ -253,7 +264,7 @@
         in_specs=[vmem],
         out_specs=vmem,
         scratch_shapes=[pltpu.VMEM((B, 2 * B), F32)],
-        compiler_params=pltpu.CompilerParams(vmem_limit_bytes=40 << 20),
+        compiler_params=pltpu.CompilerParams(vmem_limit_bytes=20 << 20),
         cost_estimate=pl.CostEstimate(
             flops=30_000_000_000, bytes_accessed=80_000_000, transcendentals=0
         ),
@@ -261,17 +272,51 @@
     )(gram)
 
 
-def apply_factor(low, home, factor):
-    nb = home.shape[1] // B
+def apply_factor(low, back, slot, factor):
+    nb = back.shape[1] // B
     vmem = pl.BlockSpec(memory_space=pltpu.VMEM)
     return pl.pallas_call(
         lambda *refs: apply_kernel(nb, factor, *refs),
-        out_shape=jax.ShapeDtypeStruct(home.shape, F32),
-        in_specs=[vmem, vmem],
+        out_shape=jax.ShapeDtypeStruct((slot.shape[0], back.shape[1]), F32),
+        in_specs=[vmem, vmem, vmem],
         out_specs=vmem,
-        compiler_params=pltpu.CompilerParams(vmem_limit_bytes=40 << 20),
+        compiler_params=pltpu.CompilerParams(vmem_limit_bytes=20 << 20),
         name="apply_factor",
-    )(low, home)
+    )(low, back, slot)
+
+
+def route_kernel(capacity, edge_ref, joining_ref, left_ref, right_ref, packed_ref, slot_ref):
+    rows = edge_ref.shape[0]
+    owners = joining_ref.shape[0]
+    table = joining_ref[...].astype(F32).astype(BF16)
+    picked = dot(hot(left_ref[...], owners).astype(BF16), table, ((1,), (0,)))
+    target = jnp.sum(picked * hot(right_ref[...], owners), axis=1, keepdims=True)
+    mine = hot(target.astype(jnp.int32), owners)
+    earlier = (
+        lax.broadcasted_iota(jnp.int32, (rows, rows), 0)
+        > lax.broadcasted_iota(jnp.int32, (rows, rows), 1)
+    ).astype(F32)
+    before = dot(earlier.astype(BF16), mine.astype(BF16), ((1,), (0,)))
+    order = jnp.sum(before * mine, axis=1, keepdims=True)
+    slot = (target * capacity + order).astype(jnp.int32)
+    slot_ref[...] = slot
+    place = hot(slot, packed_ref.shape[0]).astype(BF16)
+    packed_ref[...] = dot(place, edge_ref[...], ((0,), (0,))).astype(packed_ref.dtype)
+
+
+def route(edge_rows, joining, charge_left, charge_right, capacity):
+    rows, feature_len = edge_rows.shape
+    vmem = pl.BlockSpec(memory_space=pltpu.VMEM)
+    return pl.pallas_call(
+        lambda *refs: route_kernel(capacity, *refs),
+        out_shape=(
+            jax.ShapeDtypeStruct((joining.shape[0] * capacity, feature_len), edge_rows.dtype),
+            jax.ShapeDtypeStruct((rows, 1), jnp.int32),
+        ),
+        in_specs=[vmem] * 4,
+        out_specs=(vmem, vmem),
+        name="route",
+    )(edge_rows, joining, charge_left[:, None], charge_right[:, None])
 
 
 def per_device(edge_rows, corner, joining, charge_left, charge_right):
@@ -279,15 +324,7 @@
     owners = lax.axis_size("sec")
     capacity = 2 * row_count // owners
     factor = math.sqrt(row_count * owners)
-    target = joining[charge_left, charge_right]
-    labels = jnp.arange(owners, dtype=jnp.int32)
-    onehot = (target[:, None] == labels[None, :]).astype(jnp.int32)
-    before = jnp.cumsum(onehot, axis=0) - onehot
-    order_in = jnp.sum(before * onehot, axis=1)
-    slot_index = target * capacity + order_in
-    packed = (
-        jnp.zeros((owners * capacity, feature_len), edge_rows.dtype).at[slot_index].set(edge_rows)
-    )
+    packed, slot = route(edge_rows, joining, charge_left, charge_right, capacity)
     arrived = lax.all_to_all(
         packed.reshape(owners, capacity, feature_len),
         "sec",
@@ -305,8 +342,8 @@
         concat_axis=0,
         tiled=True,
     )
-    home_rows = returned.reshape(owners * capacity, feature_len)[slot_index]
-    return apply_factor(factor_gram(gram), home_rows, factor)
+    back = returned.reshape(owners * capacity, feature_len)
+    return apply_factor(factor_gram(gram), back, slot, factor)
 
 
 def solution(mesh):

time: 127 us -> 131 us (1.031)
  blocking collectives: 0 us -> 21.8 us
  waiting for transfers between devices: 14.5 us -> 0.01 us
  starting transfers between devices: 12.4 us -> 3.85 us
  Pallas kernels: 90.3 us -> 97.2 us
    all_to_all x0 -> x1, blocking collectives: none -> 21.8 us  [per_device(): lax.all_to_all(packed.reshape(owners, capacity, feature_len), 'sec', spli...]
    all_to_all x1 -> x0, waiting for transfers between devices: 14.5 us -> none  [per_device(): lax.all_to_all(packed.reshape(owners, capacity, feature_len), 'sec', spli...]
    all_to_all x1 -> x0, starting transfers between devices: 7.39 us -> none  [per_device(): lax.all_to_all(packed.reshape(owners, capacity, feature_len), 'sec', spli...]
    pallas_call x1, Pallas kernels: 44.4 us -> 48.3 us  [total_over_sec(): pl.pallas_call(lambda *refs: total_kernel(stages, chunks, *refs), out_sha...]
    gather x2 -> x0, local copies, waits for them, and re-layouts: 3.69 us -> none  [the longest x1 2.42 us: per_device(): home_rows = returned.reshape(owners * capacity, feature_len)[slot_index]]
    broadcast_in_dim x0 -> x2, local copies, waits for them, and re-layouts: none -> 2.78 us  [the longest x1 1.39 us: route(): charge_left[:, None]]
    pallas_call x0 -> x1, Pallas kernels: none -> 2.58 us  [route(): pl.pallas_call(lambda *refs: route_kernel(capacity, *refs), out_shape=(ja...]
    scatter x1 -> x0, local copies, waits for them, and re-layouts: 2.38 us -> none  [per_device(): jnp.zeros((owners * capacity, feature_len), edge_rows.dtype).at[slot_index]]
  transfers between devices with their start and end apart: 2 -> 1, of which waited for: 1 -> 0; matrix products, arithmetic and copies ran while one was open for 0% -> 0% of each run, Pallas kernels for 32% -> 31%
where the time goes in v5:
time: 131 us; the launch traced here: 130 us
  Pallas kernels  97.2 us (74%)
  blocking collectives  21.8 us (17%)
  local copies, waits for them, and re-layouts  7.46 us (6%)
  starting transfers between devices  3.85 us (3%)
    pallas_call x1, Pallas kernels, total_over_sec(): pl.pallas_call(lambda *refs: total_kernel(stages, chunks, *refs), out_sha...  48.3 us
    pallas_call x1, Pallas kernels, factor_gram(): pl.pallas_call(lambda *refs: factor_kernel(nb, *refs), out_shape=jax.Shap...  40.1 us
    all_to_all x1, blocking collectives, per_device(): lax.all_to_all(packed.reshape(owners, capacity, feature_len), 'sec', spli...  21.8 us
    unnamed x10, local copies, waits for them, and re-layouts  4.68 us
    all_to_all x1, starting transfers between devices, per_device(): lax.all_to_all(product.reshape(owners, capacity, feature_len), 'sec', spl...  3.85 us
    pallas_call x1, Pallas kernels, apply_factor(): pl.pallas_call(lambda *refs: apply_kernel(nb, factor, *refs), out_shape=j...  3.54 us
    pallas_call x1, Pallas kernels, products(): pl.pallas_call(lambda *refs: product_kernel(nb, *refs), out_shape=(jax.Sh...  2.63 us
  transfers between devices with their start and end apart: 1, of which 0 were waited for; matrix products, arithmetic and copies ran while one was open for 0% of the time, Pallas kernels for 31%

profile of v5, /device:TPU:0, one launch (start us, length us, event | category | flops | bytes accessed | tf_op | source)
XLA Modules:
  0.0 130.4 jit_solution(14145976106691492069)
XLA Ops:
  0.0 1.4 %copy.6.refs_2_ = s32[128,1]{1,0:T(8,128)} copy(s32[128,1]{0,1:T(1,128)} %bitcast.10) | data formatting | bytes 1024 | tf_op jit(solution)/shard_map/broadcast_in_dim | solution.py:319
  1.4 1.4 %copy.7.refs_3_ = s32[128,1]{1,0:T(8,128)} copy(s32[128,1]{0,1:T(1,128)} %bitcast.11) | data formatting | bytes 1024 | tf_op jit(solution)/shard_map/broadcast_in_dim | solution.py:319
  2.8 2.6 %route.1 = (bf16[256,1024]{1,0:T(8,128)(2,1)}, s32[128,1]{1,0:T(8,128)}) custom-call(bf16[128,1024]{1,0:T(8,128)(2,1)} %refs_0_.1, s32[16,16]{1,0:T(8,128)} %refs_1_.2, s32[128,1]{1,0:T(8,128)} %copy.6.refs_2_, s32[128,1]{1,0:T(8,128)} %copy.7.refs_3_), custom_call_target="tpu_custom_call" | custom-call | tf_op jit(solution)/shard_map/route/pallas_call | solution.py:310
  5.4 21.8 %all_to_all.10 = bf16[16,16,1024]{2,1,0:T(8,128)(2,1)S(1)} all-to-all(bf16[16,16,1024]{2,1,0:T(8,128)(2,1)} %bitcast.9), channel_id=1, replica_groups=mesh['runs'=2,'sec'=16] {'sec'}, dimensions={0} | all-to-all | bytes 1048576 | tf_op jit(solution)/shard_map/all_to_all | solution.py:328
  27.2 0.0 copy-start.2
  27.2 1.6 %copy-done.2 = bf16[1024,1024]{1,0:T(8,128)(2,1)S(1)} copy-done((bf16[1024,1024]{1,0:T(8,128)(2,1)S(1)}, bf16[1024,1024]{1,0:T(8,128)(2,1)}, u32[]{:S(2)}) %copy-start.2) | copy-done | bytes 2097176
  28.8 2.6 %products.1 = (f32[256,1024]{1,0:T(8,128)S(1)}, f32[4608,128]{1,0:T(8,128)S(1)}) custom-call(bf16[256,1024]{1,0:T(8,128)(2,1)S(1)} %bitcast.7, bf16[1024,1024]{1,0:T(8,128)(2,1)S(1)} %copy-done.2), custom_call_target="tpu_custom_call" | custom-call | tf_op jit(solution)/shard_map/products/pallas_call | solution.py:245
  31.4 0.0 copy-start.3
  31.4 48.3 %total_over_sec.1.refs_0_ = f32[4608,128]{1,0:T(8,128)S(1)} custom-call(f32[4608,128]{1,0:T(8,128)S(1)} %get-tuple-element.12.refs_0_), custom_call_target="tpu_custom_call" | custom-call | tf_op jit(solution)/shard_map/total_over_sec/pallas_call | solution.py:222
  79.8 0.0 copy-done.3
  79.8 3.8 %all-to-all-start.1 = ((f32[16,16,1024]{2,1,0:T(8,128)}), f32[16,16,1024]{2,1,0:T(8,128)S(1)}, u32[]{:S(2)}, u32[]{:S(2)}) async-start(f32[16,16,1024]{2,1,0:T(8,128)} %bitcast.8), calls=%async_computation.1 | async-start | bytes 2097152 | tf_op jit(solution)/shard_map/all_to_all | solution.py:338
  83.7 0.0 copy-start.4
  83.7 40.1 %factor_gram.1.refs_0_ = f32[4608,128]{1,0:T(8,128)S(1)} custom-call(f32[4608,128]{1,0:T(8,128)S(1)} %total_over_sec.1.refs_0_), custom_call_target="tpu_custom_call" | custom-call | flops 30000001024 | bytes 80000000 | tf_op jit(solution)/shard_map/factor_gram/pallas_call | solution.py:261
  123.8 0.0 copy-start
  123.8 1.4 %copy-done = f32[4608,128]{1,0:T(8,128)} copy-done((f32[4608,128]{1,0:T(8,128)}, f32[4608,128]{1,0:T(8,128)S(1)}, u32[]{:S(2)}) %copy-start) | copy-done | bytes 2359320
  125.2 0.0 all-to-all-done.1
  125.2 0.0 copy-done.4
  125.2 0.0 copy-start.1
  125.2 1.7 %copy-done.1 = f32[4608,128]{1,0:T(8,128)S(1)} copy-done((f32[4608,128]{1,0:T(8,128)S(1)}, f32[4608,128]{1,0:T(8,128)}, u32[]{:S(2)}) %copy-start.1) | copy-done | bytes 2359320
  126.9 3.5 %apply_factor.1 = f32[128,1024]{1,0:T(8,128)} custom-call(f32[4608,128]{1,0:T(8,128)S(1)} %copy-done.1, f32[256,1024]{1,0:T(8,128)S(1)} %bitcast.6, s32[128,1]{1,0:T(8,128)S(1)} %copy-done.4), custom_call_target="tpu_custom_call" | custom-call | tf_op jit(solution)/shard_map/apply_factor/pallas_call | solution.py:278
Async XLA Ops:
  27.2 1.6 %copy-start.2 = (bf16[1024,1024]{1,0:T(8,128)(2,1)S(1)}, bf16[1024,1024]{1,0:T(8,128)(2,1)}, u32[]{:S(2)}) copy-start(bf16[1024,1024]{1,0:T(8,128)(2,1)} %refs_1_.3) | copy-start | bytes 6291460
  31.4 48.4 %copy-start.3 = (f32[256,1024]{1,0:T(8,128)}, f32[256,1024]{1,0:T(8,128)S(1)}, u32[]{:S(2)}) copy-start(f32[256,1024]{1,0:T(8,128)S(1)} %get-tuple-element.15) | copy-start | bytes 3145732
  79.8 45.4 %all-to-all-start.1 = ((f32[16,16,1024]{2,1,0:T(8,128)}), f32[16,16,1024]{2,1,0:T(8,128)S(1)}, u32[]{:S(2)}, u32[]{:S(2)}) async-start(f32[16,16,1024]{2,1,0:T(8,128)} %bitcast.8), calls=%async_computation.1 | async-start | bytes 2097152 | tf_op jit(solution)/shard_map/all_to_all | solution.py:338
  83.7 41.6 %copy-start.4 = (s32[128,1]{1,0:T(8,128)S(1)}, s32[128,1]{1,0:T(8,128)}, u32[]{:S(2)}) copy-start(s32[128,1]{1,0:T(8,128)} %get-tuple-element.16.refs_2_) | copy-start | bytes 1540
  123.8 1.4 %copy-start = (f32[4608,128]{1,0:T(8,128)}, f32[4608,128]{1,0:T(8,128)S(1)}, u32[]{:S(2)}) copy-start(f32[4608,128]{1,0:T(8,128)S(1)} %factor_gram.1.refs_0_) | copy-start | bytes 7077892
  125.2 1.7 %copy-start.1 = (f32[4608,128]{1,0:T(8,128)S(1)}, f32[4608,128]{1,0:T(8,128)}, u32[]{:S(2)}) copy-start(f32[4608,128]{1,0:T(8,128)} %copy-done) | copy-start | bytes 7077892

commit v6 on v5

--- a/solution.py
+++ b/solution.py
@@ -116,19 +116,22 @@
 
 
 def hot(index, count):
-    lane = lax.broadcasted_iota(jnp.int32, (index.shape[0], count), 1)
-    return (lane == index).astype(F32)
-
-
-def apply_kernel(nb, factor, low_ref, back_ref, slot_ref, out_ref):
+    row = lax.broadcasted_iota(jnp.int32, (count, index.shape[1]), 0)
+    return (row == index).astype(F32)
+
+
+def apply_kernel(nb, factor, low_any, back_ref, slot_ref, out_ref, low_ref, sem):
+    copy = pltpu.make_async_copy(low_any, low_ref, sem)
+    copy.start()
     offs, _ = starts(nb)
     back = back_ref[...]
     pick = hot(slot_ref[...], back.shape[0]).astype(BF16)
     hi = back.astype(BF16)
     mid, lo = split2(back - hi.astype(F32))
-    rest = dot(pick, hi, ((1,), (0,))) + (
-        dot(pick, mid, ((1,), (0,))) + dot(pick, lo, ((1,), (0,)))
-    )
+    rest = dot(pick, hi, ((0,), (0,))) + (
+        dot(pick, mid, ((0,), (0,))) + dot(pick, lo, ((0,), (0,)))
+    )
+    copy.wait()
     for k in range(nb):
         ih, il = split2(low_ref[pl.ds(offs[k], B), :])
         xh, xl = split2(rest[:, :B])
@@ -215,7 +218,7 @@
 def total_over_sec(part, owners):
     stages = owners.bit_length() - 1
     grain = 8 * owners
-    chunks = 6 if part.shape[0] % (6 * grain) == 0 else 1
+    chunks = 3 if part.shape[0] % (3 * grain) == 0 else 1
     rows = -(-part.shape[0] // grain) * grain
     padded = jnp.pad(part, ((0, rows - part.shape[0]), (0, 0)))
     vmem = pl.BlockSpec(memory_space=pltpu.VMEM)
@@ -277,9 +280,10 @@
     vmem = pl.BlockSpec(memory_space=pltpu.VMEM)
     return pl.pallas_call(
         lambda *refs: apply_kernel(nb, factor, *refs),
-        out_shape=jax.ShapeDtypeStruct((slot.shape[0], back.shape[1]), F32),
-        in_specs=[vmem, vmem, vmem],
+        out_shape=jax.ShapeDtypeStruct((slot.shape[1], back.shape[1]), F32),
+        in_specs=[pl.BlockSpec(memory_space=pl.ANY), vmem, vmem],
         out_specs=vmem,
+        scratch_shapes=[pltpu.VMEM(low.shape, F32), pltpu.SemaphoreType.DMA],
         compiler_params=pltpu.CompilerParams(vmem_limit_bytes=20 << 20),
         name="apply_factor",
     )(low, back, slot)
@@ -289,19 +293,19 @@
     rows = edge_ref.shape[0]
     owners = joining_ref.shape[0]
     table = joining_ref[...].astype(F32).astype(BF16)
-    picked = dot(hot(left_ref[...], owners).astype(BF16), table, ((1,), (0,)))
-    target = jnp.sum(picked * hot(right_ref[...], owners), axis=1, keepdims=True)
+    picked = dot(table, hot(left_ref[...], owners).astype(BF16), ((0,), (0,)))
+    target = jnp.sum(picked * hot(right_ref[...], owners), axis=0, keepdims=True)
     mine = hot(target.astype(jnp.int32), owners)
     earlier = (
         lax.broadcasted_iota(jnp.int32, (rows, rows), 0)
-        > lax.broadcasted_iota(jnp.int32, (rows, rows), 1)
+        < lax.broadcasted_iota(jnp.int32, (rows, rows), 1)
     ).astype(F32)
-    before = dot(earlier.astype(BF16), mine.astype(BF16), ((1,), (0,)))
-    order = jnp.sum(before * mine, axis=1, keepdims=True)
+    before = dot(mine.astype(BF16), earlier.astype(BF16), ((1,), (0,)))
+    order = jnp.sum(before * mine, axis=0, keepdims=True)
     slot = (target * capacity + order).astype(jnp.int32)
     slot_ref[...] = slot
     place = hot(slot, packed_ref.shape[0]).astype(BF16)
-    packed_ref[...] = dot(place, edge_ref[...], ((0,), (0,))).astype(packed_ref.dtype)
+    packed_ref[...] = dot(place, edge_ref[...], ((1,), (0,))).astype(packed_ref.dtype)
 
 
 def route(edge_rows, joining, charge_left, charge_right, capacity):
@@ -311,12 +315,12 @@
         lambda *refs: route_kernel(capacity, *refs),
         out_shape=(
             jax.ShapeDtypeStruct((joining.shape[0] * capacity, feature_len), edge_rows.dtype),
-            jax.ShapeDtypeStruct((rows, 1), jnp.int32),
+            jax.ShapeDtypeStruct((1, rows), jnp.int32),
         ),
         in_specs=[vmem] * 4,
         out_specs=(vmem, vmem),
         name="route",
-    )(edge_rows, joining, charge_left[:, None], charge_right[:, None])
+    )(edge_rows, joining, charge_left[None, :], charge_right[None, :])
 
 
 def per_device(edge_rows, corner, joining, charge_left, charge_right):

time: 131 us -> 128 us (0.977)
  local copies, waits for them, and re-layouts: 7.46 us -> 4.65 us
    broadcast_in_dim x2 -> x0, local copies, waits for them, and re-layouts: 2.78 us -> none  [the longest x1 1.39 us: route(): charge_left[:, None]]
    unnamed x10 -> x8, local copies, waits for them, and re-layouts: 4.68 us -> 4.65 us
where the time goes in v6:
time: 128 us
  Pallas kernels  96.3 us (75%)
  blocking collectives  21.9 us (17%)
  starting transfers between devices  4.94 us (4%)
  local copies, waits for them, and re-layouts  4.65 us (4%)
    pallas_call x1, Pallas kernels, total_over_sec(): pl.pallas_call(lambda *refs: total_kernel(stages, chunks, *refs), out_sha...  47.4 us
    pallas_call x1, Pallas kernels, factor_gram(): pl.pallas_call(lambda *refs: factor_kernel(nb, *refs), out_shape=jax.Shap...  40.1 us
    all_to_all x1, blocking collectives, per_device(): lax.all_to_all(packed.reshape(owners, capacity, feature_len), 'sec', spli...  21.9 us
    all_to_all x1, starting transfers between devices, per_device(): lax.all_to_all(product.reshape(owners, capacity, feature_len), 'sec', spl...  4.94 us
    unnamed x8, local copies, waits for them, and re-layouts  4.65 us
    pallas_call x1, Pallas kernels, apply_factor(): pl.pallas_call(lambda *refs: apply_kernel(nb, factor, *refs), out_shape=j...  3.81 us
    pallas_call x1, Pallas kernels, products(): pl.pallas_call(lambda *refs: product_kernel(nb, *refs), out_shape=(jax.Sh...  2.63 us
  transfers between devices with their start and end apart: 1, of which 0 were waited for; matrix products, arithmetic and copies ran while one was open for 0% of the time, Pallas kernels for 31%

profile of v6, /device:TPU:0, one launch (start us, length us, event | category | flops | bytes accessed | tf_op | source)
XLA Modules:
  0.0 128.0 jit_solution(16696468291257985780)
XLA Ops:
  0.0 2.3 %route.1 = (bf16[256,1024]{1,0:T(8,128)(2,1)}, s32[1,128]{1,0:T(1,128)}) custom-call(bf16[128,1024]{1,0:T(8,128)(2,1)} %refs_0_.1, s32[16,16]{1,0:T(8,128)} %refs_1_.2, s32[1,128]{1,0:T(1,128)} %bitcast.9, s32[1,128]{1,0:T(1,128)} %bitcast.10), custom_call_target="tpu_custom_call" | custom-call | tf_op jit(solution)/shard_map/route/pallas_call | solution.py:314
  2.3 21.9 %all_to_all.10 = bf16[16,16,1024]{2,1,0:T(8,128)(2,1)S(1)} all-to-all(bf16[16,16,1024]{2,1,0:T(8,128)(2,1)} %bitcast.8), channel_id=1, replica_groups=mesh['runs'=2,'sec'=16] {'sec'}, dimensions={0} | all-to-all | bytes 1048576 | tf_op jit(solution)/shard_map/all_to_all | solution.py:332
  24.2 0.0 copy-start.2
  24.2 1.6 %copy-done.2 = bf16[1024,1024]{1,0:T(8,128)(2,1)S(1)} copy-done((bf16[1024,1024]{1,0:T(8,128)(2,1)S(1)}, bf16[1024,1024]{1,0:T(8,128)(2,1)}, u32[]{:S(2)}) %copy-start.2) | copy-done | bytes 2097176
  25.8 2.6 %products.1 = (f32[256,1024]{1,0:T(8,128)}, f32[4608,128]{1,0:T(8,128)S(1)}) custom-call(bf16[256,1024]{1,0:T(8,128)(2,1)S(1)} %bitcast.7, bf16[1024,1024]{1,0:T(8,128)(2,1)S(1)} %copy-done.2), custom_call_target="tpu_custom_call" | custom-call | tf_op jit(solution)/shard_map/products/pallas_call | solution.py:248
  28.4 47.4 %total_over_sec.1.refs_0_ = f32[4608,128]{1,0:T(8,128)S(1)} custom-call(f32[4608,128]{1,0:T(8,128)S(1)} %get-tuple-element.12.refs_0_), custom_call_target="tpu_custom_call" | custom-call | tf_op jit(solution)/shard_map/total_over_sec/pallas_call | solution.py:225
  75.8 0.0 copy-start
  75.9 1.4 %copy-done = f32[4608,128]{1,0:T(8,128)} copy-done((f32[4608,128]{1,0:T(8,128)}, f32[4608,128]{1,0:T(8,128)S(1)}, u32[]{:S(2)}) %copy-start) | copy-done | bytes 2359320
  77.3 4.9 %all-to-all-start.1 = ((f32[16,16,1024]{2,1,0:T(8,128)}), f32[16,16,1024]{2,1,0:T(8,128)S(1)}, u32[]{:S(2)}, u32[]{:S(2)}) async-start(f32[16,16,1024]{2,1,0:T(8,128)} %bitcast.4), calls=%async_computation.1 | async-start | bytes 2097152 | tf_op jit(solution)/shard_map/all_to_all | solution.py:342
  82.2 0.0 copy-start.1
  82.2 1.7 %copy-done.1 = f32[4608,128]{1,0:T(8,128)S(1)} copy-done((f32[4608,128]{1,0:T(8,128)S(1)}, f32[4608,128]{1,0:T(8,128)}, u32[]{:S(2)}) %copy-start.1) | copy-done | bytes 2359320
  83.9 0.0 copy-start.3
  83.9 40.1 %factor_gram.1.refs_0_ = f32[4608,128]{1,0:T(8,128)S(1)} custom-call(f32[4608,128]{1,0:T(8,128)S(1)} %copy-done.1), custom_call_target="tpu_custom_call" | custom-call | flops 30000001024 | bytes 80000000 | tf_op jit(solution)/shard_map/factor_gram/pallas_call | solution.py:264
  124.0 0.0 all-to-all-done.1
  124.0 0.0 copy-done.3
  124.0 3.8 %apply_factor.1 = f32[128,1024]{1,0:T(8,128)} custom-call(f32[4608,128]{1,0:T(8,128)S(1)} %factor_gram.1.refs_0_, f32[256,1024]{1,0:T(8,128)S(1)} %bitcast.6, s32[1,128]{1,0:T(1,128)S(1)} %copy-done.3), custom_call_target="tpu_custom_call" | custom-call | tf_op jit(solution)/shard_map/apply_factor/pallas_call | solution.py:281
Async XLA Ops:
  24.2 1.6 %copy-start.2 = (bf16[1024,1024]{1,0:T(8,128)(2,1)S(1)}, bf16[1024,1024]{1,0:T(8,128)(2,1)}, u32[]{:S(2)}) copy-start(bf16[1024,1024]{1,0:T(8,128)(2,1)} %refs_1_.3) | copy-start | bytes 6291460
  75.8 1.4 %copy-start = (f32[4608,128]{1,0:T(8,128)}, f32[4608,128]{1,0:T(8,128)S(1)}, u32[]{:S(2)}) copy-start(f32[4608,128]{1,0:T(8,128)S(1)} %total_over_sec.1.refs_0_) | copy-start | bytes 7077892
  77.3 46.7 %all-to-all-start.1 = ((f32[16,16,1024]{2,1,0:T(8,128)}), f32[16,16,1024]{2,1,0:T(8,128)S(1)}, u32[]{:S(2)}, u32[]{:S(2)}) async-start(f32[16,16,1024]{2,1,0:T(8,128)} %bitcast.4), calls=%async_computation.1 | async-start | bytes 2097152 | tf_op jit(solution)/shard_map/all_to_all | solution.py:342
  82.2 1.7 %copy-start.1 = (f32[4608,128]{1,0:T(8,128)S(1)}, f32[4608,128]{1,0:T(8,128)}, u32[]{:S(2)}) copy-start(f32[4608,128]{1,0:T(8,128)} %copy-done) | copy-start | bytes 7077892
  83.9 40.1 %copy-start.3 = (s32[1,128]{1,0:T(1,128)S(1)}, s32[1,128]{1,0:T(1,128)}, u32[]{:S(2)}) copy-start(s32[1,128]{1,0:T(1,128)} %get-tuple-element.16.refs_2_) | copy-start | bytes 1540

commit v7 on v6

--- a/solution.py
+++ b/solution.py
@@ -218,7 +218,7 @@
 def total_over_sec(part, owners):
     stages = owners.bit_length() - 1
     grain = 8 * owners
-    chunks = 3 if part.shape[0] % (3 * grain) == 0 else 1
+    chunks = 4 if part.shape[0] % (4 * grain) == 0 else 1
     rows = -(-part.shape[0] // grain) * grain
     padded = jnp.pad(part, ((0, rows - part.shape[0]), (0, 0)))
     vmem = pl.BlockSpec(memory_space=pltpu.VMEM)
@@ -234,7 +234,7 @@
             pltpu.SemaphoreType.DMA((chunks, 2 * stages)),
         ],
         compiler_params=pltpu.CompilerParams(
-            collective_id=0, has_side_effects=True, vmem_limit_bytes=20 << 20
+            collective_id=0, has_side_effects=True, vmem_limit_bytes=40 << 20
         ),
         name="total_over_sec",
     )(padded)
@@ -253,7 +253,7 @@
         ),
         in_specs=[vmem, vmem],
         out_specs=(vmem, vmem),
-        compiler_params=pltpu.CompilerParams(vmem_limit_bytes=20 << 20),
+        compiler_params=pltpu.CompilerParams(vmem_limit_bytes=48 << 20),
         name="products",
     )(rows, corner)
 
@@ -267,7 +267,7 @@
         in_specs=[vmem],
         out_specs=vmem,
         scratch_shapes=[pltpu.VMEM((B, 2 * B), F32)],
-        compiler_params=pltpu.CompilerParams(vmem_limit_bytes=20 << 20),
+        compiler_params=pltpu.CompilerParams(vmem_limit_bytes=40 << 20),
         cost_estimate=pl.CostEstimate(
             flops=30_000_000_000, bytes_accessed=80_000_000, transcendentals=0
         ),
@@ -284,7 +284,7 @@
         in_specs=[pl.BlockSpec(memory_space=pl.ANY), vmem, vmem],
         out_specs=vmem,
         scratch_shapes=[pltpu.VMEM(low.shape, F32), pltpu.SemaphoreType.DMA],
-        compiler_params=pltpu.CompilerParams(vmem_limit_bytes=20 << 20),
+        compiler_params=pltpu.CompilerParams(vmem_limit_bytes=40 << 20),
         name="apply_factor",
     )(low, back, slot)
 

time: 128 us -> 126 us (0.984)
  Pallas kernels: 96.3 us -> 95 us
    pallas_call x1, Pallas kernels: 47.4 us -> 46.1 us  [total_over_sec(): pl.pallas_call(lambda *refs: total_kernel(stages, chunks, *refs), out_sha...]
  transfers between devices with their start and end apart: 1 -> 1, of which waited for: 0 -> 0; matrix products, arithmetic and copies ran while one was open for 0% -> 0% of each run, Pallas kernels for 31% -> 32%
where the time goes in v7:
time: 126 us
  Pallas kernels  95 us (75%)
  blocking collectives  21.9 us (17%)
  local copies, waits for them, and re-layouts  4.65 us (4%)
  starting transfers between devices  3.86 us (3%)
    pallas_call x1, Pallas kernels, total_over_sec(): pl.pallas_call(lambda *refs: total_kernel(stages, chunks, *refs), out_sha...  46.1 us
    pallas_call x1, Pallas kernels, factor_gram(): pl.pallas_call(lambda *refs: factor_kernel(nb, *refs), out_shape=jax.Shap...  40.1 us
    all_to_all x1, blocking collectives, per_device(): lax.all_to_all(packed.reshape(owners, capacity, feature_len), 'sec', spli...  21.9 us
    unnamed x8, local copies, waits for them, and re-layouts  4.65 us
    all_to_all x1, starting transfers between devices, per_device(): lax.all_to_all(product.reshape(owners, capacity, feature_len), 'sec', spl...  3.86 us
    pallas_call x1, Pallas kernels, apply_factor(): pl.pallas_call(lambda *refs: apply_kernel(nb, factor, *refs), out_shape=j...  3.81 us
    pallas_call x1, Pallas kernels, products(): pl.pallas_call(lambda *refs: product_kernel(nb, *refs), out_shape=(jax.Sh...  2.63 us
  transfers between devices with their start and end apart: 1, of which 0 were waited for; matrix products, arithmetic and copies ran while one was open for 0% of the time, Pallas kernels for 32%

profile of v7, /device:TPU:0, one launch (start us, length us, event | category | flops | bytes accessed | tf_op | source)
XLA Modules:
  0.0 125.6 jit_solution(4047023197881040895)
XLA Ops:
  0.0 2.3 %route.1 = (bf16[256,1024]{1,0:T(8,128)(2,1)}, s32[1,128]{1,0:T(1,128)}) custom-call(bf16[128,1024]{1,0:T(8,128)(2,1)} %refs_0_.1, s32[16,16]{1,0:T(8,128)} %refs_1_.2, s32[1,128]{1,0:T(1,128)} %bitcast.9, s32[1,128]{1,0:T(1,128)} %bitcast.10), custom_call_target="tpu_custom_call" | custom-call | tf_op jit(solution)/shard_map/route/pallas_call | solution.py:314
  2.3 21.9 %all_to_all.10 = bf16[16,16,1024]{2,1,0:T(8,128)(2,1)S(1)} all-to-all(bf16[16,16,1024]{2,1,0:T(8,128)(2,1)} %bitcast.8), channel_id=1, replica_groups=mesh['runs'=2,'sec'=16] {'sec'}, dimensions={0} | all-to-all | bytes 1048576 | tf_op jit(solution)/shard_map/all_to_all | solution.py:332
  24.2 0.0 copy-start.2
  24.2 1.6 %copy-done.2 = bf16[1024,1024]{1,0:T(8,128)(2,1)S(1)} copy-done((bf16[1024,1024]{1,0:T(8,128)(2,1)S(1)}, bf16[1024,1024]{1,0:T(8,128)(2,1)}, u32[]{:S(2)}) %copy-start.2) | copy-done | bytes 2097176
  25.8 2.6 %products.1 = (f32[256,1024]{1,0:T(8,128)}, f32[4608,128]{1,0:T(8,128)S(1)}) custom-call(bf16[256,1024]{1,0:T(8,128)(2,1)S(1)} %bitcast.7, bf16[1024,1024]{1,0:T(8,128)(2,1)S(1)} %copy-done.2), custom_call_target="tpu_custom_call" | custom-call | tf_op jit(solution)/shard_map/products/pallas_call | solution.py:248
  28.4 46.1 %total_over_sec.1.refs_0_ = f32[4608,128]{1,0:T(8,128)S(1)} custom-call(f32[4608,128]{1,0:T(8,128)S(1)} %get-tuple-element.12.refs_0_), custom_call_target="tpu_custom_call" | custom-call | tf_op jit(solution)/shard_map/total_over_sec/pallas_call | solution.py:225
  74.5 0.0 copy-start
  74.5 1.4 %copy-done = f32[4608,128]{1,0:T(8,128)} copy-done((f32[4608,128]{1,0:T(8,128)}, f32[4608,128]{1,0:T(8,128)S(1)}, u32[]{:S(2)}) %copy-start) | copy-done | bytes 2359320
  75.9 3.9 %all-to-all-start.1 = ((f32[16,16,1024]{2,1,0:T(8,128)}), f32[16,16,1024]{2,1,0:T(8,128)S(1)}, u32[]{:S(2)}, u32[]{:S(2)}) async-start(f32[16,16,1024]{2,1,0:T(8,128)} %bitcast.4), calls=%async_computation.1 | async-start | bytes 2097152 | tf_op jit(solution)/shard_map/all_to_all | solution.py:342
  79.8 0.0 copy-start.1
  79.8 1.7 %copy-done.1 = f32[4608,128]{1,0:T(8,128)S(1)} copy-done((f32[4608,128]{1,0:T(8,128)S(1)}, f32[4608,128]{1,0:T(8,128)}, u32[]{:S(2)}) %copy-start.1) | copy-done | bytes 2359320
  81.5 0.0 copy-start.3
  81.5 40.1 %factor_gram.1.refs_0_ = f32[4608,128]{1,0:T(8,128)S(1)} custom-call(f32[4608,128]{1,0:T(8,128)S(1)} %copy-done.1), custom_call_target="tpu_custom_call" | custom-call | flops 30000001024 | bytes 80000000 | tf_op jit(solution)/shard_map/factor_gram/pallas_call | solution.py:264
  121.6 0.0 all-to-all-done.1
  121.6 0.0 copy-done.3
  121.6 3.8 %apply_factor.1 = f32[128,1024]{1,0:T(8,128)} custom-call(f32[4608,128]{1,0:T(8,128)S(1)} %factor_gram.1.refs_0_, f32[256,1024]{1,0:T(8,128)S(1)} %bitcast.6, s32[1,128]{1,0:T(1,128)S(1)} %copy-done.3), custom_call_target="tpu_custom_call" | custom-call | tf_op jit(solution)/shard_map/apply_factor/pallas_call | solution.py:281
Async XLA Ops:
  24.2 1.6 %copy-start.2 = (bf16[1024,1024]{1,0:T(8,128)(2,1)S(1)}, bf16[1024,1024]{1,0:T(8,128)(2,1)}, u32[]{:S(2)}) copy-start(bf16[1024,1024]{1,0:T(8,128)(2,1)} %refs_1_.3) | copy-start | bytes 6291460
  74.5 1.4 %copy-start = (f32[4608,128]{1,0:T(8,128)}, f32[4608,128]{1,0:T(8,128)S(1)}, u32[]{:S(2)}) copy-start(f32[4608,128]{1,0:T(8,128)S(1)} %total_over_sec.1.refs_0_) | copy-start | bytes 7077892
  75.9 45.6 %all-to-all-start.1 = ((f32[16,16,1024]{2,1,0:T(8,128)}), f32[16,16,1024]{2,1,0:T(8,128)S(1)}, u32[]{:S(2)}, u32[]{:S(2)}) async-start(f32[16,16,1024]{2,1,0:T(8,128)} %bitcast.4), calls=%async_computation.1 | async-start | bytes 2097152 | tf_op jit(solution)/shard_map/all_to_all | solution.py:342
  79.8 1.7 %copy-start.1 = (f32[4608,128]{1,0:T(8,128)S(1)}, f32[4608,128]{1,0:T(8,128)}, u32[]{:S(2)}) copy-start(f32[4608,128]{1,0:T(8,128)} %copy-done) | copy-start | bytes 7077892
  81.5 40.1 %copy-start.3 = (s32[1,128]{1,0:T(1,128)S(1)}, s32[1,128]{1,0:T(1,128)}, u32[]{:S(2)}) copy-start(s32[1,128]{1,0:T(1,128)} %get-tuple-element.16.refs_2_) | copy-start | bytes 1540
